TPU v7x, 32 devices: a whole 2x2x4 slice. The times are simulated.
32 devices in a mesh: row: 2 (over y), col: 4 (over z), depth: 4 (over x, core).
Axes of the slice: x: 2, y: 2, z: 4, core: 2. Of those that a mesh axis runs over, the one named last changes fastest.
Arguments:
- tokens: bfloat16 [512, 12288], P(('row', 'col'), 'depth'), may hold values from -6 to 6
- weight: bfloat16 [12288, 24576], P('depth', ('row', 'col')), may hold values from -5 to 5
- moment: bfloat16 [12288, 24576], P('depth', ('row', 'col')), may hold values from -0.59765625 to 0.59765625
- upstream: bfloat16 [2, 256, 24576], P(None, 'col', ('row', 'depth')), may hold values from -24 to 24
Outputs:
- activated: bfloat16 [2, 256, 24576], P(None, 'col', ('row', 'depth'))
- new_weight: bfloat16 [12288, 24576], P('depth', ('row', 'col'))
- new_moment: bfloat16 [12288, 24576], P('depth', ('row', 'col'))
All inputs are finite; a program needn't handle non-finite values.
Results may differ from a plain program's by a relative error of at most 0.015.
Values may be sent and summed in bfloat16 or wider, within the bound.
No kernel may reach another device: no remote copies, remote signals or barrier semaphores. Data moves between devices by JAX's collectives and lax.ppermute only.
A program may use at most 256 MiB of HBM per device.

v0:
```python
import jax
import jax.numpy as jnp
from jax import lax
from jax.sharding import PartitionSpec as P

D = 12288


gelu_coef = 0.7978845608028654
cubic_coef = 0.044715
lion_rate = 0.5
decay_rate = 0.1
beta_one = 0.9
beta_two = 0.99
smooth_tau = 0.1


def gelu_pair(preact):
    tangent = jnp.tanh(gelu_coef * (preact + cubic_coef * preact * preact * preact))
    gelu_value = 0.5 * preact * (1.0 + tangent)
    gelu_slope = 0.5 * (1.0 + tangent) + 0.5 * preact * (1.0 - tangent * tangent) * gelu_coef * (
        1.0 + 3.0 * cubic_coef * preact * preact
    )
    return (gelu_value, gelu_slope)


def shards(tokens, weight, moment, upstream):
    row_count = lax.axis_size("row")
    col_count = lax.axis_size("col")
    tok_rows = tokens.shape[0]
    fan_scale = D ** (-0.5)
    every_token = lax.all_gather(tokens, ("row", "col"), axis=0, tiled=True)
    token_grid = every_token.reshape(row_count, col_count, tok_rows, every_token.shape[1])
    gathered = lax.dynamic_index_in_dim(
        token_grid, lax.axis_index("col"), 1, keepdims=False
    ).reshape(row_count * tok_rows, every_token.shape[1])
    partial_value = jnp.dot(
        gathered,
        lax.all_gather(weight, "col", axis=1, tiled=True),
        preferred_element_type=jnp.float32,
    )
    summed = lax.psum_scatter(
        partial_value.astype(jnp.bfloat16), "depth", scatter_dimension=1, tiled=True
    ).astype(jnp.float32)
    gelu_value, gelu_slope = gelu_pair(summed * fan_scale)
    activated = gelu_value.astype(jnp.bfloat16)
    upstream_flat = upstream.reshape(row_count * tok_rows, upstream.shape[2]).astype(jnp.float32)
    local_grad = (upstream_flat * gelu_slope).astype(jnp.bfloat16)
    act_grad = lax.all_gather(local_grad, "depth", axis=1, tiled=True)
    moved = lax.all_to_all(act_grad, "col", split_axis=1, concat_axis=0, tiled=True)
    moved_grid = moved.reshape(col_count, row_count, tok_rows, moved.shape[1])
    grad_sum = jnp.einsum(
        "rcid,crif->df", token_grid, moved_grid, preferred_element_type=jnp.float32
    )
    grad_full = grad_sum * fan_scale
    moment_f = moment.astype(jnp.float32)
    weight_f = weight.astype(jnp.float32)
    blended = beta_one * moment_f + (1.0 - beta_one) * grad_full
    update = blended / jnp.sqrt(blended * blended + smooth_tau * smooth_tau)
    new_weight = (weight_f - lion_rate * (update + decay_rate * weight_f)).astype(jnp.bfloat16)
    new_moment = (beta_two * moment_f + (1.0 - beta_two) * grad_full).astype(jnp.bfloat16)
    activated = activated.reshape(upstream.shape[0], upstream.shape[1], activated.shape[1])
    return (activated, new_weight, new_moment)


def solution(mesh):
    placed = (
        P(("row", "col"), "depth"),
        P("depth", ("row", "col")),
        P("depth", ("row", "col")),
        P(None, "col", ("row", "depth")),
    )
    return jax.shard_map(
        shards,
        mesh=mesh,
        in_specs=placed,
        out_specs=(
            P(None, "col", ("row", "depth")),
            P("depth", ("row", "col")),
            P("depth", ("row", "col")),
        ),
        check_vma=False,
    )
```

profile of v0, /device:TPU:0, one launch (start us, length us, event | category | flops | bytes accessed | tf_op | source)
XLA Modules:
  0.0 1590.7 jit_solution(13470063521945848941)
XLA Ops:
  7.2 0.0 all-gather.4.cloned.1.call-start
  7.2 0.7 all-gather.4.cloned.1.call-update
  7.9 0.0 all-gather.6.cloned.1.call-start
  7.9 0.7 all-gather.6.cloned.1.call-update
  8.6 0.0 reduce-scatter.2.cloned.1.call-start
  8.7 64.2 %all-gather.4.cloned.1.call-done = bf16[512,3072]{1,0:T(8,128)(2,1)} async-done(((bf16[64,3072]{1,0:T(8,128)(2,1)}), bf16[512,3072]{1,0:T(8,128)(2,1)}) %all-gather.4.cloned.1.call-update) | async-done | bytes 3145744 | tf_op jit(solution)/shard_map/all_gather | solution.py:32
  72.8 1.2 constant_dynamic-slice_fusion
  74.0 1248.0 %all-gather.6.cloned.1.call-done = bf16[3072,12288]{1,0:T(8,128)(2,1)} async-done(((bf16[3072,3072]{1,0:T(8,128)(2,1)}), bf16[3072,12288]{1,0:T(8,128)(2,1)}) %all-gather.6.cloned.1.call-update) | async-done | bytes 75497488 | tf_op jit(solution)/shard_map/all_gather | solution.py:39
  1322.1 27.6 %convolution_convert_fusion = bf16[128,12288]{1,0:T(8,128)(2,1)} fusion(bf16[128,3072]{1,0:T(8,128)(2,1)S(1)} %bitcast.37, bf16[3072,12288]{1,0:T(8,128)(2,1)} %all-gather.6.cloned.1.call-done), kind=kOutput, calls=%fused_computation.13 | convolution fusion | flops 9665249280 | bytes 79429632 | tf_op jit(solution)/shard_map/dot_general | solution.py:37
  1349.6 0.0 copy-start
  1349.6 0.0 reduce-scatter.2.cloned.1.call-update
  1349.7 0.0 all-gather.8.cloned.1.call-start
  1349.7 36.1 %reduce-scatter.2.cloned.1.call-done = bf16[128,3072]{1,0:T(8,128)(2,1)} async-done(((bf16[128,12288]{1,0:T(8,128)(2,1)}), bf16[128,3072]{1,0:T(8,128)(2,1)}) %reduce-scatter.2.cloned.1.call-update) | async-done | bytes 786448 | tf_op jit(solution)/shard_map/reduce_scatter | solution.py:42
  1385.8 0.0 copy-done
  1385.8 3.5 fusion.20
  1389.3 0.0 all-gather.8.cloned.1.call-update
  1389.3 28.7 %all-gather.8.cloned.1.call-done = bf16[128,12288]{1,0:T(8,128)(2,1)} async-done(((bf16[128,3072]{1,0:T(8,128)(2,1)}), bf16[128,12288]{1,0:T(8,128)(2,1)}) %all-gather.8.cloned.1.call-update) | async-done | bytes 3145744 | tf_op jit(solution)/shard_map/all_gather | solution.py:49
  1418.0 3.8 copy.31
  1421.8 4.6 all-to-all-start
  1426.4 24.6 %copy.18 = bf16[3072,3072]{0,1:T(8,128)(2,1)} copy(bf16[3072,3072]{1,0:T(8,128)(2,1)} %param.5) | data formatting | bytes 37748736 | tf_op args[1]
  1451.0 24.6 %copy.19 = bf16[3072,3072]{0,1:T(8,128)(2,1)} copy(bf16[3072,3072]{1,0:T(8,128)(2,1)} %param.6) | data formatting | bytes 37748736 | tf_op args[2]
  1475.5 21.9 %all-to-all-done = bf16[128,4,3072]{2,0,1:T(8,128)(2,1)S(1)} async-done(((bf16[128,4,3072]{2,0,1:T(8,128)(2,1)}), bf16[128,4,3072]{2,0,1:T(8,128)(2,1)S(1)}, u32[]{:S(2)}, u32[]{:S(2)}) %all-to-all-start) | async-done | bytes 3145760 | tf_op jit(solution)/shard_map/all_to_all | solution.py:50
  1497.4 37.6 %fusion.5 = (bf16[3072,3072]{0,1:T(8,128)(2,1)}, bf16[3072,3072]{0,1:T(8,128)(2,1)}) fusion(bf16[3072,3072]{0,1:T(8,128)(2,1)} %copy.19, bf16[3072,3072]{0,1:T(8,128)(2,1)} %copy.18, bf16[4,2,64,3072]{3,2,1,0:T(8,128)(2,1)S(1)} %bitcast.38, bf16[2,4,64,3072]{3,2,1,0:T(8,128)(2,1)} %bitcast.42), kind=kOutput, calls=%fused_computation.9 | convolution fusion | flops 9824108544 | bytes 81788928 | tf_op jit(solution)/shard_map/rcid,crif->df/dot_general | solution.py:52
  1535.0 24.6 %copy.23 = bf16[3072,3072]{1,0:T(8,128)(2,1)} copy(bf16[3072,3072]{0,1:T(8,128)(2,1)} %get-tuple-element.12) | data formatting | bytes 37748736
  1559.6 24.6 %copy.22 = bf16[3072,3072]{1,0:T(8,128)(2,1)} copy(bf16[3072,3072]{0,1:T(8,128)(2,1)} %get-tuple-element.13) | data formatting | bytes 37748736
Async XLA Ops:
  7.2 65.7 %all-gather.4.cloned.1.call-start = ((), (), s32[]{:S(2)}) async-start(), calls=%async_computation.2 | async-start | bytes 3538944 | tf_op jit(solution)/shard_map/all_gather | solution.py:32
  7.9 1314.2 %all-gather.6.cloned.1.call-start = ((), (), s32[]{:S(2)}) async-start(), calls=%async_computation.3 | async-start | bytes 94371840 | tf_op jit(solution)/shard_map/all_gather | solution.py:39
  8.6 1377.1 %reduce-scatter.2.cloned.1.call-start = ((), (), s32[]{:S(2)}) async-start(), calls=%async_computation.4 | async-start | bytes 3932160 | tf_op jit(solution)/shard_map/reduce_scatter | solution.py:42
  1349.6 36.1 %copy-start = (bf16[2,64,3072]{2,1,0:T(8,128)(2,1)S(1)}, bf16[2,64,3072]{2,1,0:T(8,128)(2,1)}, u32[]{:S(2)}) copy-start(bf16[2,64,3072]{2,1,0:T(8,128)(2,1)} %param.7) | copy-start | bytes 2359300
  1349.7 68.3 %all-gather.8.cloned.1.call-start = ((), (), s32[]{:S(2)}) async-start(), calls=%async_computation.5 | async-start | bytes 3932160 | tf_op jit(solution)/shard_map/all_gather | solution.py:49
  1421.8 75.7 %all-to-all-start = ((bf16[128,4,3072]{2,0,1:T(8,128)(2,1)}), bf16[128,4,3072]{2,0,1:T(8,128)(2,1)S(1)}, u32[]{:S(2)}, u32[]{:S(2)}) async-start(bf16[128,4,3072]{2,0,1:T(8,128)(2,1)} %bitcast.36), calls=%async_computation.1 | async-start | bytes 6291456 | tf_op jit(solution)/shard_map/all_to_all | solution.py:50
Sparse Core Ops, SparseCore 0:
  10.1 62.7 all-gather.3
  74.4 1247.5 all-gather.5
  1349.8 35.9 reduce-scatter.1
  1389.4 28.4 all-gather.7
where the time goes:
time: 1590 us
  waiting for transfers between devices  1400 us (88%)
  local copies, waits for them, and re-layouts  103 us (6%)
  matrix products  65.1 us (4%)
    all_gather x1, waiting for transfers between devices, shards(): lax.all_gather(weight, 'col', axis=1, tiled=True)  1250 us
    unnamed x6, local copies, waits for them, and re-layouts  98.3 us
    all_gather x1, waiting for transfers between devices, shards(): every_token = lax.all_gather(tokens, ('row', 'col'), axis=0, tiled=True)  64.2 us
    dot_general x1, matrix products, shards(): jnp.einsum('rcid,crif->df', token_grid, moved_grid, preferred_element_typ...  37.6 us
    reduce_scatter x1, waiting for transfers between devices, shards(): lax.psum_scatter(partial_value.astype(jnp.bfloat16), 'depth', scatter_dim...  36.1 us
  transfers between devices with their start and end apart: 5, of which 5 were waited for; matrix products, arithmetic and copies ran while one was open for 3% of the time, Pallas kernels for 0%

commit v1 on v0

v1 whole, which is shorter than its diff:
```python
import functools

import jax
import jax.numpy as jnp
from jax import lax
from jax.experimental import pallas as pl
from jax.experimental.pallas import tpu as pltpu
from jax.sharding import PartitionSpec as P

gelu_coef = 0.7978845608028654
cubic_coef = 0.044715
lion_rate = 0.5
decay_rate = 0.1
beta_one = 0.9
beta_two = 0.99
smooth_tau = 0.1


def gelu_pair(preact):
    tangent = jnp.tanh(gelu_coef * (preact + cubic_coef * preact * preact * preact))
    gelu_value = 0.5 * preact * (1.0 + tangent)
    gelu_slope = 0.5 * (1.0 + tangent) + 0.5 * preact * (1.0 - tangent * tangent) * gelu_coef * (
        1.0 + 3.0 * cubic_coef * preact * preact
    )
    return (gelu_value, gelu_slope)


def tile_of(extent, unit, most):
    best = extent
    for size in range(unit, min(extent, most) + 1, unit):
        if extent % size == 0:
            best = size
    return best


def lion_kernel(strip, fan_scale, flipped, grads, weight, moment, new_weight, new_moment):
    columns = weight.shape[1]
    for start in range(0, columns, strip):
        here = slice(start, start + strip)
        grad = jnp.dot(flipped[...], grads[:, here], preferred_element_type=jnp.float32) * fan_scale
        moment_f = moment[:, here].astype(jnp.float32)
        weight_f = weight[:, here].astype(jnp.float32)
        blended = beta_one * moment_f + (1.0 - beta_one) * grad
        update = blended * lax.rsqrt(blended * blended + smooth_tau * smooth_tau)
        kept = (1.0 - lion_rate * decay_rate) * weight_f
        new_weight[:, here] = (kept - lion_rate * update).astype(new_weight.dtype)
        new_moment[:, here] = (beta_two * moment_f + (1.0 - beta_two) * grad).astype(new_moment.dtype)


def lion_step(flipped, grads, weight, moment, fan_scale):
    rows, columns = weight.shape
    count = flipped.shape[1]
    tall = tile_of(rows, 128, 256)
    strip = tile_of(columns, 128, 512)
    block = pl.BlockSpec((tall, columns), lambda i: (i, 0))
    return pl.pallas_call(
        functools.partial(lion_kernel, strip, fan_scale),
        grid=(rows // tall,),
        in_specs=[
            pl.BlockSpec((tall, count), lambda i: (i, 0)),
            pl.BlockSpec((count, columns), lambda i: (0, 0)),
            block,
            block,
        ],
        out_specs=[block, block],
        out_shape=[
            jax.ShapeDtypeStruct(weight.shape, weight.dtype),
            jax.ShapeDtypeStruct(moment.shape, moment.dtype),
        ],
        compiler_params=pltpu.CompilerParams(vmem_limit_bytes=40 * 1024 * 1024),
        cost_estimate=pl.CostEstimate(
            flops=2 * rows * columns * count,
            bytes_accessed=8 * rows * columns,
            transcendentals=rows * columns,
        ),
        name="lion_step",
    )(flipped, grads, weight, moment)


def shards(tokens, weight, moment, upstream):
    row_count = lax.axis_size("row")
    col_count = lax.axis_size("col")
    depth_count = lax.axis_size("depth")
    pieces = depth_count // col_count
    tok_rows, width = tokens.shape
    held = row_count * tok_rows
    columns = upstream.shape[2]
    fan_scale = (width * depth_count) ** (-0.5)
    swap = [
        (c * depth_count + d, (d // pieces) * depth_count + c * pieces + d % pieces)
        for c in range(col_count)
        for d in range(depth_count)
    ]
    upstream_here = lax.ppermute(upstream.reshape(held, columns), ("col", "depth"), swap)
    every_token = lax.all_gather(tokens, ("row", "col"), axis=0, tiled=True)
    ordered = (
        every_token.reshape(row_count, col_count, tok_rows, width)
        .transpose(1, 0, 2, 3)
        .reshape(col_count * held, width)
    )
    partial_value = jnp.dot(ordered, weight, preferred_element_type=jnp.float32).astype(jnp.bfloat16)
    if pieces > 1:
        partial_value = (
            partial_value.reshape(col_count, held, pieces, columns)
            .transpose(0, 2, 1, 3)
            .reshape(depth_count * held, columns)
        )
    summed = lax.psum_scatter(partial_value, "depth", scatter_dimension=0, tiled=True).astype(jnp.float32)
    gelu_value, gelu_slope = gelu_pair(summed * fan_scale)
    activated = lax.ppermute(gelu_value.astype(jnp.bfloat16), ("col", "depth"), swap)
    local_grad = (upstream_here.astype(jnp.float32) * gelu_slope).astype(jnp.bfloat16)
    act_grad = lax.all_gather(local_grad, "depth", axis=0, tiled=True)
    if pieces > 1:
        act_grad = (
            act_grad.reshape(col_count, pieces, held, columns)
            .transpose(0, 2, 1, 3)
            .reshape(col_count * held, pieces * columns)
        )
    new_weight, new_moment = lion_step(ordered.T, act_grad, weight, moment, fan_scale)
    return (activated.reshape(upstream.shape), new_weight, new_moment)


def solution(mesh):
    assert mesh.shape["depth"] % mesh.shape["col"] == 0
    placed = (
        P(("row", "col"), "depth"),
        P("depth", ("row", "col")),
        P("depth", ("row", "col")),
        P(None, "col", ("row", "depth")),
    )
    return jax.shard_map(
        shards,
        mesh=mesh,
        in_specs=placed,
        out_specs=(
            P(None, "col", ("row", "depth")),
            P("depth", ("row", "col")),
            P("depth", ("row", "col")),
        ),
        check_vma=False,
    )
```

time: 1590 us -> 231 us (0.15)
  waiting for transfers between devices: 1400 us -> 141 us
  local copies, waits for them, and re-layouts: 103 us -> 12.4 us
  matrix products: 65.1 us -> 14.9 us
  Pallas kernels: 0 us -> 35.2 us
    all_gather x2 -> x1, waiting for transfers between devices: 1280 us -> 32.2 us  [shards(): act_grad = lax.all_gather(local_grad, 'depth', axis=0, tiled=True)]
    unnamed x6 -> x7, local copies, waits for them, and re-layouts: 98.3 us -> 6.67 us
    dot_general x2 -> x1, matrix products: 65.1 us -> 14.9 us  [shards(): jnp.dot(ordered, weight, preferred_element_type=jnp.float32)]
    pallas_call x0 -> x1, Pallas kernels: none -> 35.2 us  [lion_step(): pl.pallas_call(functools.partial(lion_kernel, strip, fan_scale), grid=(ro...]
    all_to_all x1 -> x0, waiting for transfers between devices: 21.9 us -> none  [shards(): lax.all_to_all(act_grad, 'col', split_axis=1, concat_axis=0, tiled=True)]
  transfers between devices with their start and end apart: 5 -> 5, of which waited for: 5 -> 3; matrix products, arithmetic and copies ran while one was open for 3% -> 2% of each run, Pallas kernels for 0% -> 0%
where the time goes in v1:
time: 231 us; the launch traced here: 229 us
  waiting for transfers between devices  141 us (61%)
  Pallas kernels  35.2 us (15%)
  matrix products  14.9 us (6%)
  between operations  13.8 us (6%)
  local copies, waits for them, and re-layouts  12.4 us (5%)
  starting transfers between devices  8.24 us (4%)
  other arithmetic  3.49 us (2%)
    all_gather x1, waiting for transfers between devices, shards(): every_token = lax.all_gather(tokens, ('row', 'col'), axis=0, tiled=True)  64.9 us
    reduce_scatter x1, waiting for transfers between devices, shards(): lax.psum_scatter(partial_value, 'depth', scatter_dimension=0, tiled=True)  43.2 us
    pallas_call x1, Pallas kernels, lion_step(): pl.pallas_call(functools.partial(lion_kernel, strip, fan_scale), grid=(ro...  35.2 us
    all_gather x1, waiting for transfers between devices, shards(): act_grad = lax.all_gather(local_grad, 'depth', axis=0, tiled=True)  32.2 us
    dot_general x1, matrix products, shards(): jnp.dot(ordered, weight, preferred_element_type=jnp.float32)  14.9 us
    ppermute x1, starting transfers between devices, shards(): lax.ppermute(gelu_value.astype(jnp.bfloat16), ('col', 'depth'), swap)  7.43 us
    unnamed x7, local copies, waits for them, and re-layouts  6.67 us
  transfers between devices with their start and end apart: 5, of which 3 were waited for; matrix products, arithmetic and copies ran while one was open for 2% of the time, Pallas kernels for 0%

profile of v1, /device:TPU:0, one launch (start us, length us, event | category | flops | bytes accessed | tf_op | source)
XLA Modules:
  0.0 229.0 jit_solution(16923248771911781956)
XLA Ops:
  7.2 0.0 all-gather.3.cloned.1.call-start
  7.2 0.7 all-gather.3.cloned.1.call-update
  7.9 0.0 reduce-scatter.2.cloned.1.call-start
  7.9 64.9 %all-gather.3.cloned.1.call-done = bf16[512,3072]{1,0:T(8,128)(2,1)} async-done(((bf16[64,3072]{1,0:T(8,128)(2,1)}), bf16[512,3072]{1,0:T(8,128)(2,1)}) %all-gather.3.cloned.1.call-update) | async-done | bytes 3145744 | tf_op jit(solution)/shard_map/all_gather | solution.py:95
  72.8 2.2 copy.9
  75.1 0.0 copy-start.1
  75.1 1.7 copy-done.1
  76.7 14.9 %convolution_convert_fusion = bf16[512,3072]{1,0:T(8,128)(2,1)} fusion(bf16[512,3072]{1,0:T(8,128)(2,1)S(1)} %bitcast.10, bf16[3072,3072]{1,0:T(8,128)(2,1)} %weight.1), kind=kOutput, calls=%fused_computation | convolution fusion | flops 9665249280 | bytes 25165824 | tf_op jit(solution)/shard_map/dot_general | solution.py:101
  91.6 0.0 copy-start.2
  91.6 0.0 reduce-scatter.2.cloned.1.call-update
  91.7 0.0 all-gather.5.cloned.1.call-start
  91.7 1.1 copy-done.2
  92.8 0.7 collective-permute-start.1
  93.5 0.0 collective-permute-done.1
  93.5 43.2 %reduce-scatter.2.cloned.1.call-done = bf16[128,3072]{1,0:T(8,128)(2,1)} async-done(((bf16[512,3072]{1,0:T(8,128)(2,1)}), bf16[128,3072]{1,0:T(8,128)(2,1)}) %reduce-scatter.2.cloned.1.call-update) | async-done | bytes 786448 | tf_op jit(solution)/shard_map/reduce_scatter | solution.py:108
  136.7 3.5 %fusion.11 = (bf16[128,3072]{1,0:T(8,128)(2,1)}, bf16[128,3072]{1,0:T(8,128)(2,1)}) fusion(bf16[128,3072]{1,0:T(8,128)(2,1)} %reduce-scatter.2.cloned.1.call-done, bf16[128,3072]{1,0:T(8,128)(2,1)S(1)} %collective-permute-done.1), kind=kLoop, calls=%fused_computation.16 | loop fusion | flops 9437184 | bytes 3145728 | tf_op jit(solution)/shard_map/convert_element_type | solution.py:111
  140.2 0.0 all-gather.5.cloned.1.call-update
  140.2 7.4 %collective-permute-start = (bf16[128,3072]{1,0:T(8,128)(2,1)}, bf16[128,3072]{1,0:T(8,128)(2,1)}, u32[]{:S(2)}, u32[]{:S(2)}) collective-permute-start(bf16[128,3072]{1,0:T(8,128)(2,1)} %get-tuple-element.8), channel_id=1, source_target_pairs={{0,0},{1,4},{2,8},{3,12},{4,1},{5,5},{6,9},{7,13},{8,2},{9,6},{10,... | collective-permute-start | bytes 2359304 | tf_op jit(solution)/shard_map/ppermute | solution.py:110
  147.6 3.5 %copy.10 = bf16[512,3072]{0,1:T(8,128)(2,1)S(1)} copy(bf16[512,3072]{1,0:T(8,128)(2,1)} %bitcast.11) | data formatting | bytes 6291456 | tf_op jit(solution)/shard_map/reshape | solution.py:99
  151.2 0.0 collective-permute-done
  151.2 32.2 %all-gather.5.cloned.1.call-done.grads = bf16[512,3072]{1,0:T(8,128)(2,1)} async-done(((bf16[128,3072]{1,0:T(8,128)(2,1)}), bf16[512,3072]{1,0:T(8,128)(2,1)}) %all-gather.5.cloned.1.call-update) | async-done | bytes 3145744 | tf_op jit(solution)/shard_map/all_gather | solution.py:112
  183.3 0.0 copy-start
  183.3 1.9 copy-done
  185.2 35.2 %lion_step.1 = (bf16[3072,3072]{1,0:T(8,128)(2,1)}, bf16[3072,3072]{1,0:T(8,128)(2,1)}) custom-call(bf16[3072,512]{1,0:T(8,128)(2,1)S(1)} %bitcast.9, bf16[512,3072]{1,0:T(8,128)(2,1)S(1)} %copy-done, bf16[3072,3072]{1,0:T(8,128)(2,1)} %weight.1, bf16[3072,3072]{1,0:T(8,128)(2,1)} %moment.1), custom_call_target="tpu_custom_call" | custom-call | flops 9663676416 | bytes 75497472 | tf_op jit(solution)/shard_map/lion_step/pallas_call | solution.py:56
  220.4 2.1 copy.12
Async XLA Ops:
  7.2 65.7 %all-gather.3.cloned.1.call-start = ((), (), s32[]{:S(2)}) async-start(), calls=%async_computation.1 | async-start | bytes 3538944 | tf_op jit(solution)/shard_map/all_gather | solution.py:95
  7.9 128.8 %reduce-scatter.2.cloned.1.call-start = ((), (), s32[]{:S(2)}) async-start(), calls=%async_computation.2 | async-start | bytes 3932160 | tf_op jit(solution)/shard_map/reduce_scatter | solution.py:108
  75.1 1.7 copy-start.1
  91.6 1.1 copy-start.2
  91.7 91.7 %all-gather.5.cloned.1.call-start = ((), (), s32[]{:S(2)}) async-start(), calls=%async_computation.3 | async-start | bytes 3932160 | tf_op jit(solution)/shard_map/all_gather | solution.py:112
  92.8 0.7 collective-permute-start.1
  140.2 11.0 %collective-permute-start = (bf16[128,3072]{1,0:T(8,128)(2,1)}, bf16[128,3072]{1,0:T(8,128)(2,1)}, u32[]{:S(2)}, u32[]{:S(2)}) collective-permute-start(bf16[128,3072]{1,0:T(8,128)(2,1)} %get-tuple-element.8), channel_id=1, source_target_pairs={{0,0},{1,4},{2,8},{3,12},{4,1},{5,5},{6,9},{7,13},{8,2},{9,6},{10,... | collective-permute-start | bytes 2359304 | tf_op jit(solution)/shard_map/ppermute | solution.py:110
  183.3 1.9 copy-start
Sparse Core Ops, SparseCore 0:
  10.1 62.7 all-gather.2
  91.8 44.8 reduce-scatter.1
  140.3 42.9 all-gather.4

commit v2 on v1

v2 whole, which is shorter than its diff:
```python
import functools

import jax
import jax.numpy as jnp
from jax import lax
from jax.experimental import pallas as pl
from jax.experimental.pallas import tpu as pltpu
from jax.sharding import PartitionSpec as P


gelu_coef = 0.7978845608028654
cubic_coef = 0.044715
lion_rate = 0.5
decay_rate = 0.1
beta_one = 0.9
beta_two = 0.99
smooth_tau = 0.1


def gelu_pair(preact):
    tangent = jnp.tanh(gelu_coef * (preact + cubic_coef * preact * preact * preact))
    gelu_value = 0.5 * preact * (1.0 + tangent)
    gelu_slope = 0.5 * (1.0 + tangent) + 0.5 * preact * (1.0 - tangent * tangent) * gelu_coef * (
        1.0 + 3.0 * cubic_coef * preact * preact
    )
    return (gelu_value, gelu_slope)


def tile_of(extent, unit, most):
    best = extent
    for size in range(unit, min(extent, most) + 1, unit):
        if extent % size == 0:
            best = size
    return best


def reverse_bits(value, bits):
    return sum(((value >> b) & 1) << (bits - 1 - b) for b in range(bits))


def fetch_kernel(parts, source, target, sems):
    tall = source.shape[0] // parts
    copies = [
        pltpu.make_async_copy(
            source.at[pl.ds(i * tall, tall)], target.at[pl.ds(i * tall, tall)], sems.at[i]
        )
        for i in range(parts)
    ]
    for copy in copies:
        copy.start()
    for copy in copies:
        copy.wait()


def fetch(value):
    parts = 4
    return pl.pallas_call(
        functools.partial(fetch_kernel, parts),
        in_specs=[pl.BlockSpec(memory_space=pltpu.HBM)],
        out_specs=pl.BlockSpec(memory_space=pltpu.VMEM),
        out_shape=pltpu.VMEM(value.shape, value.dtype),
        scratch_shapes=[pltpu.SemaphoreType.DMA((parts,))],
        compiler_params=pltpu.CompilerParams(vmem_limit_bytes=1024 * 1024),
        cost_estimate=pl.CostEstimate(flops=0, bytes_accessed=value.size * 2, transcendentals=0),
    )(pltpu.with_memory_space_constraint(value, pltpu.HBM))


def order_kernel(wanted, *refs):
    col_count = lax.axis_size("col")
    blocks, (ordered, flipped) = refs[:-2], refs[-2:]
    tall = blocks[0].shape[0]
    for j, which in enumerate(wanted()):
        away = lax.rem(which - lax.axis_index("col") + col_count, col_count)
        for o, block in enumerate(blocks):

            @pl.when(away == o)
            def _(j=j, block=block):
                ordered[j * tall : (j + 1) * tall, :] = block[...]

    width = ordered.shape[1]
    wide = tile_of(width, 128, 256)
    for start in range(0, width, wide):
        flipped[start : start + wide, :] = ordered[:, start : start + wide].T


def order_tokens(wanted, blocks):
    tall, width = blocks[0].shape
    count = tall * len(blocks)
    kind = blocks[0].dtype
    whole = pl.BlockSpec(memory_space=pltpu.VMEM)
    return pl.pallas_call(
        functools.partial(order_kernel, wanted),
        in_specs=[whole] * len(blocks),
        out_specs=[whole, whole],
        out_shape=[pltpu.VMEM((count, width), kind), pltpu.VMEM((width, count), kind)],
        compiler_params=pltpu.CompilerParams(vmem_limit_bytes=12 * 1024 * 1024),
        cost_estimate=pl.CostEstimate(flops=0, bytes_accessed=6 * count * width, transcendentals=0),
        name="order_tokens",
    )(*blocks)


def lion_kernel(shape, strip, fan_scale, *refs):
    chunks, pieces = shape
    flipped, held = refs[:chunks], refs[chunks : chunks * (1 + pieces)]
    weight, moment, new_weight, new_moment, grads = refs[chunks * (1 + pieces) :]
    tall = held[0].shape[0]

    @pl.when(pl.program_id(0) == 0)
    def _():
        for i, piece in enumerate(held):
            grads[i * tall : (i + 1) * tall, :] = piece[...]

    count = tall * pieces
    kind = new_weight.dtype
    for start in range(0, new_weight.shape[1], strip):
        here = slice(start, start + strip)
        grad = sum(
            jnp.dot(f[...], grads[j * count : (j + 1) * count, here], preferred_element_type=jnp.float32)
            for j, f in enumerate(flipped)
        )
        old, kept = moment[:, here], weight[:, here]
        change = (grad * fan_scale).astype(kind) - old
        blended = old + jnp.asarray(1.0 - beta_one, kind) * change
        update = blended * lax.rsqrt(blended * blended + jnp.asarray(smooth_tau * smooth_tau, kind))
        new_weight[:, here] = kept - jnp.asarray(lion_rate, kind) * (update + jnp.asarray(decay_rate, kind) * kept)
        new_moment[:, here] = old + jnp.asarray(1.0 - beta_two, kind) * change


def lion_step(flipped, held, weight, moment, fan_scale):
    rows, columns = weight.shape
    tall = tile_of(rows, 128, 256)
    strip = tile_of(columns, 128, 512)
    block = pl.BlockSpec((tall, columns), lambda i: (i, 0))
    parts = [piece for chunk in held for piece in chunk]
    count = sum(f.shape[1] for f in flipped)
    return pl.pallas_call(
        functools.partial(lion_kernel, (len(held), len(held[0])), strip, fan_scale),
        grid=(rows // tall,),
        in_specs=[pl.BlockSpec((tall, f.shape[1]), lambda i: (i, 0)) for f in flipped]
        + [pl.BlockSpec(p.shape, lambda i: (0, 0), pipeline_mode=pl.Buffered(1)) for p in parts]
        + [block, block],
        out_specs=[block, block],
        out_shape=[
            jax.ShapeDtypeStruct(weight.shape, weight.dtype),
            jax.ShapeDtypeStruct(moment.shape, moment.dtype),
        ],
        scratch_shapes=[pltpu.VMEM((count, columns), weight.dtype)],
        compiler_params=pltpu.CompilerParams(vmem_limit_bytes=40 * 1024 * 1024),
        cost_estimate=pl.CostEstimate(
            flops=2 * rows * columns * count,
            bytes_accessed=8 * rows * columns,
            transcendentals=rows * columns,
        ),
        name="lion_step",
    )(*flipped, *parts, weight, moment)


def shards(tokens, weight, moment, upstream):
    row_count = lax.axis_size("row")
    col_count = lax.axis_size("col")
    depth_count = lax.axis_size("depth")
    row, depth = lax.axis_index("row"), lax.axis_index("depth")
    pieces = depth_count // col_count
    bits = depth_count.bit_length() - 1
    tok_rows, width = tokens.shape
    columns = upstream.shape[2]
    fan_scale = (width * depth_count) ** (-0.5)

    near = fetch(weight)

    if pieces == 1:
        set_of, part_of = [reverse_bits(q, bits) for q in range(depth_count)], [0] * depth_count
    else:
        set_of = [q // pieces for q in range(depth_count)]
        part_of = [q % pieces for q in range(depth_count)]
    piece_at = {(set_of[q], part_of[q]): q for q in range(depth_count)}
    home = [
        (c * depth_count + q, set_of[q] * depth_count + c * pieces + part_of[q])
        for c in range(col_count)
        for q in range(depth_count)
    ]
    away = [(b, a) for a, b in home]
    order = [reverse_bits(j, bits) for j in range(depth_count)]

    def wanted():
        if pieces > 1:
            return [jnp.int32(t) for t in range(col_count)]
        here = lax.axis_index("depth")
        return [
            sum(((here ^ q) >> b & 1) << (bits - 1 - b) for b in range(bits)) for q in order
        ]

    def flip(value, bit):
        return lax.ppermute(value, "depth", [(q, q ^ (1 << bit)) for q in range(depth_count)])

    up = [(c, (c + 1) % col_count) for c in range(col_count)]
    down = [(b, a) for a, b in up]
    ring = [(r, (r - 1) % row_count) for r in range(row_count)]

    first = {0: tokens}
    from_above = from_below = tokens
    for step in range(1, (col_count + 1) // 2):
        from_above = lax.ppermute(from_above, "col", down)
        from_below = lax.ppermute(from_below, "col", up)
        first[step], first[col_count - step] = from_above, from_below
    if col_count > 1 and col_count % 2 == 0:
        half = tok_rows // 2
        first[col_count // 2] = jnp.concatenate(
            [lax.ppermute(from_above[:half], "col", down), lax.ppermute(from_below[half:], "col", up)]
        )
    upstream, _ = lax.optimization_barrier((upstream, first[col_count // 2]))
    blocks = [[first[o] for o in range(col_count)]]
    for _ in range(1, row_count):
        blocks.append([lax.ppermute(b, "row", ring) for b in blocks[-1]])

    flipped, grads, values = [], [], []
    for j in range(row_count):
        ordered, turned = order_tokens(wanted, blocks[j])
        if pieces == 1:
            count = ordered.shape[0] // 2
            sent = jnp.dot(ordered[count:], near, preferred_element_type=jnp.float32).astype(jnp.bfloat16)
            kept = jnp.dot(ordered[:count], near, preferred_element_type=jnp.float32)
        else:
            partial_value = jnp.dot(ordered, near, preferred_element_type=jnp.float32)
            partial_value = partial_value.reshape(col_count, tok_rows, pieces, columns).transpose(0, 2, 1, 3)
            partial_value = jnp.concatenate(
                [
                    lax.dynamic_index_in_dim(
                        partial_value.reshape(depth_count, tok_rows, columns), depth ^ q, 0, keepdims=False
                    )
                    for q in order
                ]
            )
            count = partial_value.shape[0] // 2
            sent, kept = partial_value[count:].astype(jnp.bfloat16), partial_value[:count]
        for bit in range(bits):
            kept = kept + flip(sent, bit).astype(jnp.float32)
            if bit + 1 < bits:
                count = kept.shape[0] // 2
                sent, kept = kept[count:].astype(jnp.bfloat16), kept[:count]
        gelu_value, gelu_slope = gelu_pair(kept * fan_scale)
        values.append(lax.ppermute(gelu_value.astype(jnp.bfloat16), ("col", "depth"), home))
        theirs = lax.dynamic_index_in_dim(upstream, lax.rem(row + j, row_count), 0, keepdims=False)
        theirs = lax.ppermute(theirs, ("col", "depth"), away).astype(jnp.float32)
        held = [(theirs * gelu_slope).astype(jnp.bfloat16)]
        for bit in reversed(range(bits)):
            held = held + [flip(h, bit) for h in held]
        if pieces > 1:
            stacked = jnp.stack(held)
            table = jnp.array([order.index(q) for q in range(depth_count)], jnp.int32)
            grad = jnp.stack(
                [
                    lax.dynamic_index_in_dim(stacked, table[depth ^ piece_at[t, p]], 0, keepdims=False)
                    for t in range(col_count)
                    for p in range(pieces)
                ]
            )
            grad = grad.reshape(col_count, pieces, tok_rows, columns).transpose(0, 2, 1, 3)
            held = [grad.reshape(col_count * tok_rows, pieces * columns)]
        flipped.append(turned)
        grads.append(held)
    new_weight, new_moment = lion_step(flipped, grads, weight, moment, fan_scale)
    twice = jnp.stack(values + values)
    activated = lax.dynamic_slice_in_dim(twice, row_count - row, row_count, axis=0)
    return (activated, new_weight, new_moment)


def solution(mesh):
    depth_count, col_count = mesh.shape["depth"], mesh.shape["col"]
    assert depth_count % col_count == 0 and depth_count & (depth_count - 1) == 0
    placed = (
        P(("row", "col"), "depth"),
        P("depth", ("row", "col")),
        P("depth", ("row", "col")),
        P(None, "col", ("row", "depth")),
    )

    return jax.shard_map(
        shards,
        mesh=mesh,
        in_specs=placed,
        out_specs=(
            P(None, "col", ("row", "depth")),
            P("depth", ("row", "col")),
            P("depth", ("row", "col")),
        ),
        check_vma=False,
    )
```

time: 231 us -> 160 us (0.69)
  waiting for transfers between devices: 141 us -> 48.6 us
  starting transfers between devices: 8.24 us -> 34.5 us
  between operations: 13.8 us -> 0.82 us
  Pallas kernels: 35.2 us -> 43 us
  matrix products: 14.9 us -> 19.4 us
  local copies, waits for them, and re-layouts: 12.4 us -> 7.99 us
    all_gather x2 -> x0, waiting for transfers between devices: 97.1 us -> none  [the longest x1 64.9 us: shards(): every_token = lax.all_gather(tokens, ('row', 'col'), axis=0, tiled=True)]
    ppermute x2 -> x22, waiting for transfers between devices: 0.01 us -> 48.6 us  [the longest x10 33.4 us: flip(): lax.ppermute(value, 'depth', [(q, q ^ 1 << bit) for q in range(depth_coun...]
    reduce_scatter x1 -> x0, waiting for transfers between devices: 43.2 us -> none  [shards(): lax.psum_scatter(partial_value, 'depth', scatter_dimension=0, tiled=True)]
    ppermute x2 -> x22, starting transfers between devices: 8.13 us -> 34.5 us  [the longest x10 11.5 us: flip(): lax.ppermute(value, 'depth', [(q, q ^ 1 << bit) for q in range(depth_coun...]
    pallas_call x1 -> x4, Pallas kernels: 35.2 us -> 43 us  [the longest x1 35.1 us: lion_step(): pl.pallas_call(functools.partial(lion_kernel, (len(held), len(held[0])),...]
    dot_general x1 -> x4, matrix products: 14.9 us -> 19.4 us  [the longest x2 12.8 us: shards(): jnp.dot(ordered[count:], near, preferred_element_type=jnp.float32)]
    reshape x1 -> x0, local copies, waits for them, and re-layouts: 3.52 us -> none  [shards(): ordered = every_token.reshape(row_count, col_count, tok_rows, width).tran...]
    another operation x0 -> x1, other arithmetic: none -> 2.77 us  [shards(): twice = jnp.stack(values + values)]
  transfers between devices with their start and end apart: 5 -> 22, of which waited for: 3 -> 5; matrix products, arithmetic and copies ran while one was open for 2% -> 16% of each run, Pallas kernels for 0% -> 5%
where the time goes in v2:
time: 160 us; the launch traced here: 159 us
  waiting for transfers between devices  48.6 us (30%)
  Pallas kernels  43 us (27%)
  starting transfers between devices  34.5 us (22%)
  matrix products  19.4 us (12%)
  local copies, waits for them, and re-layouts  7.99 us (5%)
  other arithmetic  4.8 us (3%)
    pallas_call x1, Pallas kernels, lion_step(): pl.pallas_call(functools.partial(lion_kernel, (len(held), len(held[0])),...  35.1 us
    ppermute x10, waiting for transfers between devices, flip(): lax.ppermute(value, 'depth', [(q, q ^ 1 << bit) for q in range(depth_coun...  33.4 us
    dot_general x2, matrix products, shards(): jnp.dot(ordered[count:], near, preferred_element_type=jnp.float32)  12.8 us
    ppermute x10, starting transfers between devices, flip(): lax.ppermute(value, 'depth', [(q, q ^ 1 << bit) for q in range(depth_coun...  11.5 us
    ppermute x1, waiting for transfers between devices, shards(): from_above = lax.ppermute(from_above, 'col', down)  9.82 us
    unnamed x13, local copies, waits for them, and re-layouts  6.88 us
    dot_general x2, matrix products, shards(): kept = jnp.dot(ordered[:count], near, preferred_element_type=jnp.float32)  6.61 us
    pallas_call x1, Pallas kernels, fetch(): pl.pallas_call(functools.partial(fetch_kernel, parts), in_specs=[pl.Block...  6.49 us
  transfers between devices with their start and end apart: 22, of which 5 were waited for; matrix products, arithmetic and copies ran while one was open for 16% of the time, Pallas kernels for 5%

profile of v2, /device:TPU:0, one launch (start us, length us, event | category | flops | bytes accessed | tf_op | source)
XLA Modules:
  0.0 159.3 jit_solution(1201865780424763002)
XLA Ops:
  0.6 5.1 %collective-permute-start = (bf16[64,3072]{1,0:T(8,128)(2,1)}, bf16[64,3072]{1,0:T(8,128)(2,1)S(1)}, u32[]{:S(2)}, u32[]{:S(2)}) collective-permute-start(bf16[64,3072]{1,0:T(8,128)(2,1)} %refs_0_.1), channel_id=1, source_target_pairs={{4,0},{8,4},{12,8},{0,12},{5,1},{9,5},{13,9},{1,13},{6,2},{10,6},{... | collective-permute-start | bytes 1179656 | tf_op jit(solution)/shard_map/ppermute | solution.py:203
  5.8 0.0 collective-permute-start.2
  5.8 9.8 %collective-permute-done.refs_1_ = bf16[64,3072]{1,0:T(8,128)(2,1)S(1)} collective-permute-done((bf16[64,3072]{1,0:T(8,128)(2,1)}, bf16[64,3072]{1,0:T(8,128)(2,1)S(1)}, u32[]{:S(2)}, u32[]{:S(2)}) %collective-permute-start) | collective-permute-done | bytes 393248 | tf_op jit(solution)/shard_map/ppermute | solution.py:203
  15.6 4.2 %collective-permute-start.1 = (bf16[32,3072]{1,0:T(8,128)(2,1)S(1)}, bf16[32,3072]{1,0:T(8,128)(2,1)S(1)}, u32[]{:S(2)}, u32[]{:S(2)}) collective-permute-start(bf16[32,3072]{1,0:T(8,128)(2,1)S(1)} %slice.42), channel_id=1, source_target_pairs={{4,0},{8,4},{12,8},{0,12},{5,1},{9,5},{13,9},{1,13},{6,2},{10,6},{... | collective-permute-start | bytes 589832 | tf_op jit(solution)/shard_map/ppermute | solution.py:209
  19.8 1.5 collective-permute-start.7
  21.4 6.5 %shard_map.67 = bf16[3072,3072]{1,0:T(8,128)(2,1)S(1)} custom-call(bf16[3072,3072]{1,0:T(8,128)(2,1)} %refs_10_.1), custom_call_target="tpu_custom_call" | custom-call | bytes 18874368 | tf_op jit(solution)/shard_map/pallas_call | solution.py:57
  27.9 0.0 copy-start
  27.9 6.8 %copy-done = bf16[3072,3072]{1,0:T(8,128)(2,1)} copy-done((bf16[3072,3072]{1,0:T(8,128)(2,1)}, bf16[3072,3072]{1,0:T(8,128)(2,1)S(1)}, u32[]{:S(2)}) %copy-start) | copy-done | bytes 18874392
  34.7 0.0 collective-permute-done.2.refs_3_
  34.7 0.1 collective-permute-start.3
  34.8 0.6 collective-permute-start.10
  35.4 1.5 collective-permute-start.8
  36.9 0.0 collective-permute-done.1
  36.9 5.3 %collective-permute-done.3 = bf16[32,3072]{1,0:T(8,128)(2,1)S(1)} collective-permute-done((bf16[32,3072]{1,0:T(8,128)(2,1)S(1)}, bf16[32,3072]{1,0:T(8,128)(2,1)S(1)}, u32[]{:S(2)}, u32[]{:S(2)}) %collective-permute-start.3) | collective-permute-done | bytes 196640 | tf_op jit(solution)/shard_map/ppermute | solution.py:209
  42.3 0.6 collective-permute-start.9
  42.8 0.0 copy-done.5
  42.8 1.0 dynamic-slice_bitcast_fusion
  43.8 1.6 %collective-permute-start.18 = (bf16[64,3072]{1,0:T(8,128)(2,1)}, bf16[64,3072]{1,0:T(8,128)(2,1)S(1)}, u32[]{:S(2)}, u32[]{:S(2)}) collective-permute-start(bf16[64,3072]{1,0:T(8,128)(2,1)} %get-tuple-element.21), channel_id=1, source_target_pairs={{0,0},{8,1},{4,2},{12,3},{1,4},{9,5},{5,6},{13,7},{2,8},{10,9},{6,... | collective-permute-start | bytes 1179656 | tf_op jit(solution)/shard_map/ppermute | solution.py:244
  45.5 0.0 copy-done.4
  45.5 0.6 order_tokens.2
  46.1 0.0 copy-start.1
  46.1 10.1 %convolution_convert_fusion.1 = bf16[128,3072]{1,0:T(8,128)(2,1)} fusion(bf16[3072,3072]{1,0:T(8,128)(2,1)} %copy-done, bf16[256,3072]{1,0:T(8,128)(2,1)S(1)} %get-tuple-element.10), kind=kOutput, calls=%fused_computation.3 | convolution fusion | flops 2416312320 | bytes 20447232 | tf_op jit(solution)/shard_map/dot_general | solution.py:221
  56.2 0.0 collective-permute-done.7.refs_0_
  56.2 1.9 %collective-permute-start.14 = (bf16[64,3072]{1,0:T(8,128)(2,1)}, bf16[64,3072]{1,0:T(8,128)(2,1)S(1)}, u32[]{:S(2)}, u32[]{:S(2)}) collective-permute-start(bf16[64,3072]{1,0:T(8,128)(2,1)} %get-tuple-element.22), channel_id=1, source_target_pairs={{0,0},{8,1},{4,2},{12,3},{1,4},{9,5},{5,6},{13,7},{2,8},{10,9},{6,... | collective-permute-start | bytes 1179656 | tf_op jit(solution)/shard_map/ppermute | solution.py:244
  58.1 0.0 collective-permute-done.10.refs_3_
  58.1 3.7 %collective-permute-start.4 = (bf16[128,3072]{1,0:T(8,128)(2,1)}, bf16[128,3072]{1,0:T(8,128)(2,1)}, u32[]{:S(2)}, u32[]{:S(2)}) collective-permute-start(bf16[128,3072]{1,0:T(8,128)(2,1)} %convolution_convert_fusion.1), channel_id=1, source_target_pairs={{0,1},{1,0},{2,3},{3,2},{4,5},{5,4},{6,7},{7,6},{8,9},{9,8},{10,11... | collective-permute-start | bytes 2359304 | tf_op jit(solution)/shard_map/ppermute | solution.py:194
  61.8 0.0 collective-permute-done.8.refs_1_
  61.8 0.0 collective-permute-done.9.refs_2_
  61.8 0.8 order_tokens.3
  62.6 0.0 copy-start.2
  62.6 0.0 copy-done.1
  62.6 2.8 %convolution_convert_fusion = bf16[128,3072]{1,0:T(8,128)(2,1)S(1)} fusion(bf16[3072,3072]{1,0:T(8,128)(2,1)S(1)} %copy-done.1, bf16[256,3072]{1,0:T(8,128)(2,1)S(1)} %get-tuple-element.11), kind=kOutput, calls=%fused_computation.2 | convolution fusion | flops 2416312320 | bytes 20447232 | tf_op jit(solution)/shard_map/dot_general | solution.py:221
  65.4 0.0 copy-done.2
  65.4 0.1 collective-permute-start.11
  65.5 0.0 collective-permute-done.4
  65.5 3.9 %convolution_add_fusion.1 = f32[128,3072]{1,0:T(8,128)S(1)} fusion(bf16[3072,3072]{1,0:T(8,128)(2,1)S(1)} %copy-done.1, bf16[128,3072]{1,0:T(8,128)(2,1)} %collective-permute-done.4, bf16[256,3072]{1,0:T(8,128)(2,1)S(1)} %get-tuple-element.10), kind=kOutput, calls=%fused_computation.1 | convolution fusion | flops 2416705536 | bytes 22020096 | tf_op jit(solution)/shard_map/dot_general | solution.py:222
  69.5 0.1 collective-permute-start.5
  69.6 0.0 collective-permute-done.11
  69.6 2.7 %convolution_add_fusion = f32[128,3072]{1,0:T(8,128)S(1)} fusion(bf16[3072,3072]{1,0:T(8,128)(2,1)S(1)} %copy-done.1, bf16[128,3072]{1,0:T(8,128)(2,1)S(1)} %collective-permute-done.11, bf16[256,3072]{1,0:T(8,128)(2,1)S(1)} %get-tuple-element.11), kind=kOutput, calls=%fused_computation | convolution fusion | flops 2416705536 | bytes 22020096 | tf_op jit(solution)/shard_map/dot_general | solution.py:222
  72.3 2.1 %collective-permute-start.12 = (bf16[64,3072]{1,0:T(8,128)(2,1)S(1)}, bf16[64,3072]{1,0:T(8,128)(2,1)S(1)}, u32[]{:S(2)}, u32[]{:S(2)}) collective-permute-start(bf16[64,3072]{1,0:T(8,128)(2,1)S(1)} %slice.68), channel_id=1, source_target_pairs={{0,2},{1,3},{2,0},{3,1},{4,6},{5,7},{6,4},{7,5},{8,10},{9,11},{10,... | collective-permute-start | bytes 1179656 | tf_op jit(solution)/shard_map/ppermute | solution.py:194
  74.4 0.0 collective-permute-done.14
  74.4 7.1 %collective-permute-done.5 = bf16[64,3072]{1,0:T(8,128)(2,1)S(1)} collective-permute-done((bf16[64,3072]{1,0:T(8,128)(2,1)S(1)}, bf16[64,3072]{1,0:T(8,128)(2,1)S(1)}, u32[]{:S(2)}, u32[]{:S(2)}) %collective-permute-start.5) | collective-permute-done | bytes 393248 | tf_op jit(solution)/shard_map/ppermute | solution.py:194
  81.5 0.6 multiply_convert_fusion.1
  82.2 1.4 collective-permute-start.6
  83.6 2.4 %collective-permute-start.15 = (bf16[64,3072]{1,0:T(8,128)(2,1)S(1)}, bf16[64,3072]{1,0:T(8,128)(2,1)S(1)}, u32[]{:S(2)}, u32[]{:S(2)}) collective-permute-start(bf16[64,3072]{1,0:T(8,128)(2,1)S(1)} %get-tuple-element.19.refs_2_), channel_id=1, source_target_pairs={{0,2},{1,3},{2,0},{3,1},{4,6},{5,7},{6,4},{7,5},{8,10},{9,11},{10,... | collective-permute-start | bytes 1179656 | tf_op jit(solution)/shard_map/ppermute | solution.py:194
  86.0 0.0 collective-permute-done.18
  86.0 10.1 %collective-permute-done.12 = bf16[64,3072]{1,0:T(8,128)(2,1)S(1)} collective-permute-done((bf16[64,3072]{1,0:T(8,128)(2,1)S(1)}, bf16[64,3072]{1,0:T(8,128)(2,1)S(1)}, u32[]{:S(2)}, u32[]{:S(2)}) %collective-permute-start.12) | collective-permute-done | bytes 393248 | tf_op jit(solution)/shard_map/ppermute | solution.py:194
  96.1 1.4 multiply_convert_fusion
  97.4 2.5 %collective-permute-start.19 = (bf16[64,3072]{1,0:T(8,128)(2,1)S(1)}, bf16[64,3072]{1,0:T(8,128)(2,1)S(1)}, u32[]{:S(2)}, u32[]{:S(2)}) collective-permute-start(bf16[64,3072]{1,0:T(8,128)(2,1)S(1)} %get-tuple-element.17.refs_6_), channel_id=1, source_target_pairs={{0,2},{1,3},{2,0},{3,1},{4,6},{5,7},{6,4},{7,5},{8,10},{9,11},{10,... | collective-permute-start | bytes 1179656 | tf_op jit(solution)/shard_map/ppermute | solution.py:194
  100.0 4.5 %collective-permute-start.13 = (bf16[64,3072]{1,0:T(8,128)(2,1)}, bf16[64,3072]{1,0:T(8,128)(2,1)}, u32[]{:S(2)}, u32[]{:S(2)}) collective-permute-start(bf16[64,3072]{1,0:T(8,128)(2,1)} %get-tuple-element.18), channel_id=1, source_target_pairs={{0,0},{1,8},{2,4},{3,12},{4,1},{5,9},{6,5},{7,13},{8,2},{9,10},{10... | collective-permute-start | bytes 1179656 | tf_op jit(solution)/shard_map/ppermute | solution.py:242
  104.5 0.0 collective-permute-start.16
  104.5 0.0 collective-permute-done.6
  104.5 0.5 collective-permute-start.20
  105.0 0.0 collective-permute-done.15.refs_3_
  105.0 0.1 collective-permute-start.17
  105.1 16.2 %collective-permute-done.19.refs_7_ = bf16[64,3072]{1,0:T(8,128)(2,1)S(1)} collective-permute-done((bf16[64,3072]{1,0:T(8,128)(2,1)S(1)}, bf16[64,3072]{1,0:T(8,128)(2,1)S(1)}, u32[]{:S(2)}, u32[]{:S(2)}) %collective-permute-start.19) | collective-permute-done | bytes 393248 | tf_op jit(solution)/shard_map/ppermute | solution.py:194
  121.3 0.0 collective-permute-start.21
  121.3 0.0 collective-permute-done.13
  121.3 2.8 %fusion.6 = bf16[2,64,3072]{2,1,0:T(8,128)(2,1)} fusion(s32[]{:T(128)S(6)} %select_n.10, bf16[1,64,3072]{2,1,0:T(8,128)(2,1)} %bitcast, bf16[1,64,3072]{2,1,0:T(8,128)(2,1)} %bitcast.1), kind=kLoop, calls=%fused_computation.16 | loop fusion | flops 1179648 | bytes 1572868 | tf_op jit(solution)/shard_map/stack | solution.py:263
  124.1 0.0 collective-permute-done.16.refs_4_
  124.1 0.0 collective-permute-done.17.refs_5_
  124.1 0.0 collective-permute-done.20.refs_8_
  124.1 0.0 collective-permute-done.21.refs_9_
  124.1 35.1 %lion_step.1 = (bf16[3072,3072]{1,0:T(8,128)(2,1)}, bf16[3072,3072]{1,0:T(8,128)(2,1)}) custom-call(bf16[3072,256]{1,0:T(8,128)(2,1)S(1)} %get-tuple-element.12.refs_0_, bf16[3072,256]{1,0:T(8,128)(2,1)S(1)} %copy-done.3, bf16[64,3072]{1,0:T(8,128)(2,1)S(1)} %get-tuple-element.19.refs_2_, bf16[64,3072]{1,0:T(8,128)(2,1)S(1)} %collective-permute-done.15.refs_3_, ...), custom_call_target="tpu_custom_call" | custom-call | flops 9663676416 | bytes 75497472 | tf_op jit(solution)/shard_map/lion_step/pallas_call | solution.py:136
  (10 shorter events, 0.1 us)
Async XLA Ops:
  0.6 15.0 %collective-permute-start = (bf16[64,3072]{1,0:T(8,128)(2,1)}, bf16[64,3072]{1,0:T(8,128)(2,1)S(1)}, u32[]{:S(2)}, u32[]{:S(2)}) collective-permute-start(bf16[64,3072]{1,0:T(8,128)(2,1)} %refs_0_.1), channel_id=1, source_target_pairs={{4,0},{8,4},{12,8},{0,12},{5,1},{9,5},{13,9},{1,13},{6,2},{10,6},{... | collective-permute-start | bytes 1179656 | tf_op jit(solution)/shard_map/ppermute | solution.py:203
  5.8 29.0 %collective-permute-start.2 = (bf16[64,3072]{1,0:T(8,128)(2,1)}, bf16[64,3072]{1,0:T(8,128)(2,1)S(1)}, u32[]{:S(2)}, u32[]{:S(2)}) collective-permute-start(bf16[64,3072]{1,0:T(8,128)(2,1)} %refs_0_.1), channel_id=1, source_target_pairs={{0,4},{4,8},{8,12},{12,0},{1,5},{5,9},{9,13},{13,1},{2,6},{6,10},{... | collective-permute-start | bytes 1179656 | tf_op jit(solution)/shard_map/ppermute | solution.py:204
  15.6 21.3 %collective-permute-start.1 = (bf16[32,3072]{1,0:T(8,128)(2,1)S(1)}, bf16[32,3072]{1,0:T(8,128)(2,1)S(1)}, u32[]{:S(2)}, u32[]{:S(2)}) collective-permute-start(bf16[32,3072]{1,0:T(8,128)(2,1)S(1)} %slice.42), channel_id=1, source_target_pairs={{4,0},{8,4},{12,8},{0,12},{5,1},{9,5},{13,9},{1,13},{6,2},{10,6},{... | collective-permute-start | bytes 589832 | tf_op jit(solution)/shard_map/ppermute | solution.py:209
  19.8 36.4 %collective-permute-start.7 = (bf16[64,3072]{1,0:T(8,128)(2,1)}, bf16[64,3072]{1,0:T(8,128)(2,1)S(1)}, u32[]{:S(2)}, u32[]{:S(2)}) collective-permute-start(bf16[64,3072]{1,0:T(8,128)(2,1)} %refs_0_.1), channel_id=1, source_target_pairs={{0,16},{16,0},{1,17},{17,1},{2,18},{18,2},{3,19},{19,3},{4,20},{20... | collective-permute-start | bytes 1179656 | tf_op jit(solution)/shard_map/ppermute | solution.py:214
  27.9 6.9 %copy-start = (bf16[3072,3072]{1,0:T(8,128)(2,1)}, bf16[3072,3072]{1,0:T(8,128)(2,1)S(1)}, u32[]{:S(2)}) copy-start(bf16[3072,3072]{1,0:T(8,128)(2,1)S(1)} %shard_map.67) | copy-start | bytes 56623108
  34.7 8.1 %copy-start.5 = (bf16[2,64,3072]{2,1,0:T(8,128)(2,1)S(1)}, bf16[2,64,3072]{2,1,0:T(8,128)(2,1)}, u32[]{:S(2)}) copy-start(bf16[2,64,3072]{2,1,0:T(8,128)(2,1)} %param.7) | copy-start | bytes 2359300
  34.7 10.8 %copy-start.4 = (bf16[64,3072]{1,0:T(8,128)(2,1)S(1)}, bf16[64,3072]{1,0:T(8,128)(2,1)}, u32[]{:S(2)}) copy-start(bf16[64,3072]{1,0:T(8,128)(2,1)} %refs_0_.1) | copy-start | bytes 1179652
  34.7 7.5 %collective-permute-start.3 = (bf16[32,3072]{1,0:T(8,128)(2,1)S(1)}, bf16[32,3072]{1,0:T(8,128)(2,1)S(1)}, u32[]{:S(2)}, u32[]{:S(2)}) collective-permute-start(bf16[32,3072]{1,0:T(8,128)(2,1)S(1)} %slice.43), channel_id=1, source_target_pairs={{0,4},{4,8},{8,12},{12,0},{1,5},{5,9},{9,13},{13,1},{2,6},{6,10},{... | collective-permute-start | bytes 589832 | tf_op jit(solution)/shard_map/ppermute | solution.py:209
  34.8 23.3 %collective-permute-start.10 = (bf16[64,3072]{1,0:T(8,128)(2,1)S(1)}, bf16[64,3072]{1,0:T(8,128)(2,1)S(1)}, u32[]{:S(2)}, u32[]{:S(2)}) collective-permute-start(bf16[64,3072]{1,0:T(8,128)(2,1)S(1)} %collective-permute-done.2.refs_3_), channel_id=1, source_target_pairs={{0,16},{16,0},{1,17},{17,1},{2,18},{18,2},{3,19},{19,3},{4,20},{20... | collective-permute-start | bytes 1179656 | tf_op jit(solution)/shard_map/ppermute | solution.py:214
  35.4 26.4 %collective-permute-start.8 = (bf16[64,3072]{1,0:T(8,128)(2,1)S(1)}, bf16[64,3072]{1,0:T(8,128)(2,1)S(1)}, u32[]{:S(2)}, u32[]{:S(2)}) collective-permute-start(bf16[64,3072]{1,0:T(8,128)(2,1)S(1)} %collective-permute-done.refs_1_), channel_id=1, source_target_pairs={{0,16},{16,0},{1,17},{17,1},{2,18},{18,2},{3,19},{19,3},{4,20},{20... | collective-permute-start | bytes 1179656 | tf_op jit(solution)/shard_map/ppermute | solution.py:214
  42.3 19.5 %collective-permute-start.9 = (bf16[64,3072]{1,0:T(8,128)(2,1)S(1)}, bf16[64,3072]{1,0:T(8,128)(2,1)S(1)}, u32[]{:S(2)}, u32[]{:S(2)}) collective-permute-start(bf16[64,3072]{1,0:T(8,128)(2,1)S(1)} %constant_dynamic-update-slice_fusion.refs_2_), channel_id=1, source_target_pairs={{0,16},{16,0},{1,17},{17,1},{2,18},{18,2},{3,19},{19,3},{4,20},{20... | collective-permute-start | bytes 1179656 | tf_op jit(solution)/shard_map/ppermute | solution.py:214
  43.8 42.2 %collective-permute-start.18 = (bf16[64,3072]{1,0:T(8,128)(2,1)}, bf16[64,3072]{1,0:T(8,128)(2,1)S(1)}, u32[]{:S(2)}, u32[]{:S(2)}) collective-permute-start(bf16[64,3072]{1,0:T(8,128)(2,1)} %get-tuple-element.21), channel_id=1, source_target_pairs={{0,0},{8,1},{4,2},{12,3},{1,4},{9,5},{5,6},{13,7},{2,8},{10,9},{6,... | collective-permute-start | bytes 1179656 | tf_op jit(solution)/shard_map/ppermute | solution.py:244
  46.1 16.5 %copy-start.1 = (bf16[3072,3072]{1,0:T(8,128)(2,1)S(1)}, bf16[3072,3072]{1,0:T(8,128)(2,1)}, u32[]{:S(2)}) copy-start(bf16[3072,3072]{1,0:T(8,128)(2,1)} %copy-done) | copy-start | bytes 56623108
  56.2 18.2 %collective-permute-start.14 = (bf16[64,3072]{1,0:T(8,128)(2,1)}, bf16[64,3072]{1,0:T(8,128)(2,1)S(1)}, u32[]{:S(2)}, u32[]{:S(2)}) collective-permute-start(bf16[64,3072]{1,0:T(8,128)(2,1)} %get-tuple-element.22), channel_id=1, source_target_pairs={{0,0},{8,1},{4,2},{12,3},{1,4},{9,5},{5,6},{13,7},{2,8},{10,9},{6,... | collective-permute-start | bytes 1179656 | tf_op jit(solution)/shard_map/ppermute | solution.py:244
  58.1 7.4 %collective-permute-start.4 = (bf16[128,3072]{1,0:T(8,128)(2,1)}, bf16[128,3072]{1,0:T(8,128)(2,1)}, u32[]{:S(2)}, u32[]{:S(2)}) collective-permute-start(bf16[128,3072]{1,0:T(8,128)(2,1)} %convolution_convert_fusion.1), channel_id=1, source_target_pairs={{0,1},{1,0},{2,3},{3,2},{4,5},{5,4},{6,7},{7,6},{8,9},{9,8},{10,11... | collective-permute-start | bytes 2359304 | tf_op jit(solution)/shard_map/ppermute | solution.py:194
  62.6 2.8 %copy-start.2 = (bf16[3072,256]{1,0:T(8,128)(2,1)}, bf16[3072,256]{1,0:T(8,128)(2,1)S(1)}, u32[]{:S(2)}) copy-start(bf16[3072,256]{1,0:T(8,128)(2,1)S(1)} %get-tuple-element.13.refs_1_) | copy-start | bytes 4718596
  65.4 4.2 %collective-permute-start.11 = (bf16[128,3072]{1,0:T(8,128)(2,1)S(1)}, bf16[128,3072]{1,0:T(8,128)(2,1)S(1)}, u32[]{:S(2)}, u32[]{:S(2)}) collective-permute-start(bf16[128,3072]{1,0:T(8,128)(2,1)S(1)} %convolution_convert_fusion), channel_id=1, source_target_pairs={{0,1},{1,0},{2,3},{3,2},{4,5},{5,4},{6,7},{7,6},{8,9},{9,8},{10,11... | collective-permute-start | bytes 2359304 | tf_op jit(solution)/shard_map/ppermute | solution.py:194
  69.5 12.1 %collective-permute-start.5 = (bf16[64,3072]{1,0:T(8,128)(2,1)S(1)}, bf16[64,3072]{1,0:T(8,128)(2,1)S(1)}, u32[]{:S(2)}, u32[]{:S(2)}) collective-permute-start(bf16[64,3072]{1,0:T(8,128)(2,1)S(1)} %slice.69), channel_id=1, source_target_pairs={{0,2},{1,3},{2,0},{3,1},{4,6},{5,7},{6,4},{7,5},{8,10},{9,11},{10,... | collective-permute-start | bytes 1179656 | tf_op jit(solution)/shard_map/ppermute | solution.py:194
  72.3 23.7 %collective-permute-start.12 = (bf16[64,3072]{1,0:T(8,128)(2,1)S(1)}, bf16[64,3072]{1,0:T(8,128)(2,1)S(1)}, u32[]{:S(2)}, u32[]{:S(2)}) collective-permute-start(bf16[64,3072]{1,0:T(8,128)(2,1)S(1)} %slice.68), channel_id=1, source_target_pairs={{0,2},{1,3},{2,0},{3,1},{4,6},{5,7},{6,4},{7,5},{8,10},{9,11},{10,... | collective-permute-start | bytes 1179656 | tf_op jit(solution)/shard_map/ppermute | solution.py:194
  82.2 22.3 %collective-permute-start.6 = (bf16[64,3072]{1,0:T(8,128)(2,1)S(1)}, bf16[64,3072]{1,0:T(8,128)(2,1)}, u32[]{:S(2)}, u32[]{:S(2)}) collective-permute-start(bf16[64,3072]{1,0:T(8,128)(2,1)S(1)} %get-tuple-element.20), channel_id=1, source_target_pairs={{0,0},{1,8},{2,4},{3,12},{4,1},{5,9},{6,5},{7,13},{8,2},{9,10},{10... | collective-permute-start | bytes 1179656 | tf_op jit(solution)/shard_map/ppermute | solution.py:242
  83.6 21.4 %collective-permute-start.15 = (bf16[64,3072]{1,0:T(8,128)(2,1)S(1)}, bf16[64,3072]{1,0:T(8,128)(2,1)S(1)}, u32[]{:S(2)}, u32[]{:S(2)}) collective-permute-start(bf16[64,3072]{1,0:T(8,128)(2,1)S(1)} %get-tuple-element.19.refs_2_), channel_id=1, source_target_pairs={{0,2},{1,3},{2,0},{3,1},{4,6},{5,7},{6,4},{7,5},{8,10},{9,11},{10,... | collective-permute-start | bytes 1179656 | tf_op jit(solution)/shard_map/ppermute | solution.py:194
  97.4 23.9 %collective-permute-start.19 = (bf16[64,3072]{1,0:T(8,128)(2,1)S(1)}, bf16[64,3072]{1,0:T(8,128)(2,1)S(1)}, u32[]{:S(2)}, u32[]{:S(2)}) collective-permute-start(bf16[64,3072]{1,0:T(8,128)(2,1)S(1)} %get-tuple-element.17.refs_6_), channel_id=1, source_target_pairs={{0,2},{1,3},{2,0},{3,1},{4,6},{5,7},{6,4},{7,5},{8,10},{9,11},{10,... | collective-permute-start | bytes 1179656 | tf_op jit(solution)/shard_map/ppermute | solution.py:194
  100.0 21.4 %collective-permute-start.13 = (bf16[64,3072]{1,0:T(8,128)(2,1)}, bf16[64,3072]{1,0:T(8,128)(2,1)}, u32[]{:S(2)}, u32[]{:S(2)}) collective-permute-start(bf16[64,3072]{1,0:T(8,128)(2,1)} %get-tuple-element.18), channel_id=1, source_target_pairs={{0,0},{1,8},{2,4},{3,12},{4,1},{5,9},{6,5},{7,13},{8,2},{9,10},{10... | collective-permute-start | bytes 1179656 | tf_op jit(solution)/shard_map/ppermute | solution.py:242
  104.5 19.6 %collective-permute-start.16 = (bf16[64,3072]{1,0:T(8,128)(2,1)S(1)}, bf16[64,3072]{1,0:T(8,128)(2,1)S(1)}, u32[]{:S(2)}, u32[]{:S(2)}) collective-permute-start(bf16[64,3072]{1,0:T(8,128)(2,1)S(1)} %get-tuple-element.19.refs_2_), channel_id=1, source_target_pairs={{0,1},{1,0},{2,3},{3,2},{4,5},{5,4},{6,7},{7,6},{8,9},{9,8},{10,11... | collective-permute-start | bytes 1179656 | tf_op jit(solution)/shard_map/ppermute | solution.py:194
  104.5 19.6 %collective-permute-start.20 = (bf16[64,3072]{1,0:T(8,128)(2,1)S(1)}, bf16[64,3072]{1,0:T(8,128)(2,1)}, u32[]{:S(2)}, u32[]{:S(2)}) collective-permute-start(bf16[64,3072]{1,0:T(8,128)(2,1)S(1)} %get-tuple-element.17.refs_6_), channel_id=1, source_target_pairs={{0,1},{1,0},{2,3},{3,2},{4,5},{5,4},{6,7},{7,6},{8,9},{9,8},{10,11... | collective-permute-start | bytes 1179656 | tf_op jit(solution)/shard_map/ppermute | solution.py:194
  105.0 19.1 %collective-permute-start.17 = (bf16[64,3072]{1,0:T(8,128)(2,1)S(1)}, bf16[64,3072]{1,0:T(8,128)(2,1)}, u32[]{:S(2)}, u32[]{:S(2)}) collective-permute-start(bf16[64,3072]{1,0:T(8,128)(2,1)S(1)} %collective-permute-done.15.refs_3_), channel_id=1, source_target_pairs={{0,1},{1,0},{2,3},{3,2},{4,5},{5,4},{6,7},{7,6},{8,9},{9,8},{10,11... | collective-permute-start | bytes 1179656 | tf_op jit(solution)/shard_map/ppermute | solution.py:194
  121.3 2.8 %collective-permute-start.21 = (bf16[64,3072]{1,0:T(8,128)(2,1)S(1)}, bf16[64,3072]{1,0:T(8,128)(2,1)}, u32[]{:S(2)}, u32[]{:S(2)}) collective-permute-start(bf16[64,3072]{1,0:T(8,128)(2,1)S(1)} %collective-permute-done.19.refs_7_), channel_id=1, source_target_pairs={{0,1},{1,0},{2,3},{3,2},{4,5},{5,4},{6,7},{7,6},{8,9},{9,8},{10,11... | collective-permute-start | bytes 1179656 | tf_op jit(solution)/shard_map/ppermute | solution.py:194
  121.3 2.8 %copy-start.3 = (bf16[3072,256]{1,0:T(8,128)(2,1)S(1)}, bf16[3072,256]{1,0:T(8,128)(2,1)}, u32[]{:S(2)}) copy-start(bf16[3072,256]{1,0:T(8,128)(2,1)} %copy-done.2) | copy-start | bytes 4718596

commit v3 on v2

v3 whole, which is shorter than its diff:
```python
import functools

import jax
import jax.numpy as jnp
from jax import lax
from jax.experimental import pallas as pl
from jax.experimental.pallas import tpu as pltpu
from jax.sharding import PartitionSpec as P


near = pl.BlockSpec(memory_space=pltpu.VMEM)

gelu_coef = 0.7978845608028654
cubic_coef = 0.044715
lion_rate = 0.5
decay_rate = 0.1
beta_one = 0.9
beta_two = 0.99
smooth_tau = 0.1


def gelu_pair(preact):
    tangent = jnp.tanh(gelu_coef * (preact + cubic_coef * preact * preact * preact))
    gelu_value = 0.5 * preact * (1.0 + tangent)
    gelu_slope = 0.5 * (1.0 + tangent) + 0.5 * preact * (1.0 - tangent * tangent) * gelu_coef * (
        1.0 + 3.0 * cubic_coef * preact * preact
    )
    return (gelu_value, gelu_slope)


def tile_of(extent, unit, most):
    best = extent
    for size in range(unit, min(extent, most) + 1, unit):
        if extent % size == 0:
            best = size
    return best


def reverse_bits(value, bits):
    return sum(((value >> b) & 1) << (bits - 1 - b) for b in range(bits))


def far(value):
    return pltpu.with_memory_space_constraint(value, pltpu.HBM)


def mix_kernel(wanted, *refs):
    col_count = lax.axis_size("col")
    *blocks, weight, flipped, kept, sent, ordered, stored, sems = refs
    tall = blocks[0].shape[0]
    _, width = ordered.shape
    parts, _, strip = stored.shape
    copies = [
        pltpu.make_async_copy(weight.at[:, pl.ds(i * strip, strip)], stored.at[i], sems.at[i])
        for i in range(parts)
    ]
    for copy in copies:
        copy.start()
    for j, which in enumerate(wanted()):
        away = lax.rem(which - lax.axis_index("col") + col_count, col_count)
        for o, block in enumerate(blocks):

            @pl.when(away == o)
            def _(j=j, block=block):
                ordered[j * tall : (j + 1) * tall, :] = block[...]

    wide = tile_of(width, 128, 256)
    for start in range(0, width, wide):
        flipped[start : start + wide, :] = ordered[:, start : start + wide].T

    rows = kept.shape[0]
    for i in range(parts):
        copies[i].wait()
        here = slice(i * strip, (i + 1) * strip)
        value = jnp.dot(ordered[...], stored[i], preferred_element_type=jnp.float32)
        kept[:, here] = value[:rows]
        sent[:, here] = value[rows:].astype(sent.dtype)


def mix(wanted, blocks, weight):
    tall, width = blocks[0].shape
    count = tall * len(blocks)
    columns = weight.shape[1]
    kind = weight.dtype
    strip = tile_of(columns, 128, 512)
    parts = columns // strip
    return pl.pallas_call(
        functools.partial(mix_kernel, wanted),
        in_specs=[near] * len(blocks) + [pl.BlockSpec(memory_space=pltpu.HBM)],
        out_specs=[near] * 3,
        out_shape=[
            jax.ShapeDtypeStruct((width, count), kind),
            jax.ShapeDtypeStruct((count // 2, columns), jnp.float32),
            jax.ShapeDtypeStruct((count // 2, columns), kind),
        ],
        scratch_shapes=[
            pltpu.VMEM((count, width), kind),
            pltpu.VMEM((parts, width, strip), kind),
            pltpu.SemaphoreType.DMA((parts,)),
        ],
        compiler_params=pltpu.CompilerParams(vmem_limit_bytes=32 * 1024 * 1024),
        cost_estimate=pl.CostEstimate(
            flops=2 * count * width * columns, bytes_accessed=2 * width * columns, transcendentals=0
        ),
        name="mix",
    )(*blocks, far(weight))


def fold_kernel(strip, old, arrived, kept, sent):
    half = kept.shape[0]
    for start in range(0, old.shape[1], strip):
        here = slice(start, start + strip)
        value = old[:, here] + arrived[:, here].astype(jnp.float32)
        kept[:, here] = value[:half]
        sent[:, here] = value[half:].astype(sent.dtype)


def fold(old, arrived):
    rows, columns = arrived.shape
    return pl.pallas_call(
        functools.partial(fold_kernel, tile_of(columns, 128, 256)),
        out_shape=[
            jax.ShapeDtypeStruct((rows // 2, columns), jnp.float32),
            jax.ShapeDtypeStruct((rows // 2, columns), arrived.dtype),
        ],
        compiler_params=pltpu.CompilerParams(vmem_limit_bytes=8 * 1024 * 1024),
        cost_estimate=pl.CostEstimate(flops=rows * columns, bytes_accessed=8 * rows * columns, transcendentals=0),
        name="fold",
    )(old, arrived)


def slope_kernel(strip, fan_scale, kept, arrived, upstream, value, grad):
    for start in range(0, kept.shape[1], strip):
        here = slice(start, start + strip)
        preact = (kept[:, here] + arrived[:, here].astype(jnp.float32)) * fan_scale
        gelu_value, gelu_slope = gelu_pair(preact)
        value[:, here] = gelu_value.astype(value.dtype)
        grad[:, here] = (upstream[:, here].astype(jnp.float32) * gelu_slope * fan_scale).astype(grad.dtype)


def slope(kept, arrived, upstream, fan_scale):
    shape, kind = arrived.shape, arrived.dtype
    return pl.pallas_call(
        functools.partial(slope_kernel, tile_of(shape[1], 128, 256), fan_scale),
        out_shape=[jax.ShapeDtypeStruct(shape, kind)] * 2,
        compiler_params=pltpu.CompilerParams(vmem_limit_bytes=8 * 1024 * 1024),
        cost_estimate=pl.CostEstimate(
            flops=30 * shape[0] * shape[1], bytes_accessed=0, transcendentals=shape[0] * shape[1]
        ),
        name="slope",
    )(kept, arrived, upstream)


def lion_kernel(shape, strip, *refs):
    chunks, pieces = shape
    flipped, held = refs[:chunks], refs[chunks : chunks * (1 + pieces)]
    weight, moment, new_weight, new_moment, left, grads, weights, moments, sems = refs[chunks * (1 + pieces) :]
    tall = left.shape[0]
    steps = weights.shape[0] // tall
    kind = weights.dtype

    def copies(step, back):
        rows = pl.ds(pl.multiple_of(step * tall, tall), tall)
        pairs = ((weights, new_weight), (moments, new_moment)) if back else ((weight, weights), (moment, moments))
        return [
            pltpu.make_async_copy(a.at[rows], b.at[rows], sems.at[2 * back + k, step])
            for k, (a, b) in enumerate(pairs)
        ]

    @pl.loop(0, steps)
    def _(step):
        for copy in copies(step, 0):
            copy.start()

    high = held[0].shape[0]
    for i, piece in enumerate(held):
        grads[i * high : (i + 1) * high, :] = piece[...]
    count = high * pieces

    @pl.loop(0, steps)
    def _(step):
        for copy in copies(step, 0):
            copy.wait()
        rows = pl.ds(pl.multiple_of(step * tall, tall), tall)
        for j, f in enumerate(flipped):
            left[:, j * count : (j + 1) * count] = f[rows, :]
        for start in range(0, weights.shape[1], strip):
            here = slice(start, start + strip)
            grad = jnp.dot(left[...], grads[:, here], preferred_element_type=jnp.float32).astype(kind)
            old, kept = moments[rows, here], weights[rows, here]
            change = grad - old
            blended = old + jnp.asarray(1.0 - beta_one, kind) * change
            update = blended * lax.rsqrt(blended * blended + jnp.asarray(smooth_tau * smooth_tau, kind))
            weights[rows, here] = kept - jnp.asarray(lion_rate, kind) * (
                update + jnp.asarray(decay_rate, kind) * kept
            )
            moments[rows, here] = old + jnp.asarray(1.0 - beta_two, kind) * change
        for copy in copies(step, 1):
            copy.start()

    @pl.loop(0, steps)
    def _(step):
        for copy in copies(step, 1):
            copy.wait()


def lion_step(flipped, held, weight, moment):
    rows, columns = weight.shape
    tall = tile_of(rows, 128, 256)
    strip = tile_of(columns, 128, 256)
    parts = [piece for chunk in held for piece in chunk]
    count = sum(f.shape[1] for f in flipped)
    there = pl.BlockSpec(memory_space=pltpu.HBM)
    kind = weight.dtype
    return pl.pallas_call(
        functools.partial(lion_kernel, (len(held), len(held[0])), strip),
        in_specs=[near] * (len(flipped) + len(parts)) + [there] * 2,
        out_specs=[there] * 2,
        out_shape=[
            jax.ShapeDtypeStruct(weight.shape, weight.dtype),
            jax.ShapeDtypeStruct(moment.shape, moment.dtype),
        ],
        scratch_shapes=[
            pltpu.VMEM((tall, count), kind),
            pltpu.VMEM((count, columns), kind),
            pltpu.VMEM((rows, columns), kind),
            pltpu.VMEM((rows, columns), kind),
            pltpu.SemaphoreType.DMA((4, rows // tall)),
        ],
        compiler_params=pltpu.CompilerParams(vmem_limit_bytes=54 * 1024 * 1024),
        cost_estimate=pl.CostEstimate(
            flops=2 * rows * columns * count,
            bytes_accessed=8 * rows * columns,
            transcendentals=rows * columns,
        ),
        name="lion_step",
    )(*flipped, *parts, far(weight), far(moment))


def shards(tokens, weight, moment, upstream):
    row_count = lax.axis_size("row")
    col_count = lax.axis_size("col")
    depth_count = lax.axis_size("depth")
    row, depth = lax.axis_index("row"), lax.axis_index("depth")
    pieces = depth_count // col_count
    bits = depth_count.bit_length() - 1
    tok_rows, width = tokens.shape
    columns = upstream.shape[2]
    fan_scale = (width * depth_count) ** (-0.5)

    if pieces == 1:
        set_of, part_of = [reverse_bits(q, bits) for q in range(depth_count)], [0] * depth_count
    else:
        set_of = [q // pieces for q in range(depth_count)]
        part_of = [q % pieces for q in range(depth_count)]
    piece_at = {(set_of[q], part_of[q]): q for q in range(depth_count)}
    home = [
        (c * depth_count + q, set_of[q] * depth_count + c * pieces + part_of[q])
        for c in range(col_count)
        for q in range(depth_count)
    ]
    away = [(b, a) for a, b in home]
    order = [reverse_bits(j, bits) for j in range(depth_count)]

    def wanted():
        if pieces > 1:
            return [jnp.int32(t) for t in range(col_count)]
        here = lax.axis_index("depth")
        return [
            sum(((here ^ q) >> b & 1) << (bits - 1 - b) for b in range(bits)) for q in order
        ]

    def flip(value, bit):
        return lax.ppermute(value, "depth", [(q, q ^ (1 << bit)) for q in range(depth_count)])

    up = [(c, (c + 1) % col_count) for c in range(col_count)]
    down = [(b, a) for a, b in up]
    ring = [(r, (r - 1) % row_count) for r in range(row_count)]

    first = {0: tokens}
    from_above = from_below = tokens
    for step in range(1, (col_count + 1) // 2):
        from_above = lax.ppermute(from_above, "col", down)
        from_below = lax.ppermute(from_below, "col", up)
        first[step], first[col_count - step] = from_above, from_below
    if col_count > 1 and col_count % 2 == 0:
        half = tok_rows // 2
        above_half = lax.ppermute(from_above[:half], "col", down)
        below_half = lax.ppermute(from_below[half:], "col", up)
        first[col_count // 2] = jnp.concatenate([above_half, below_half])
    blocks = [[first[o] for o in range(col_count)]]
    for _ in range(1, row_count):
        passed = []
        for block in blocks[-1]:
            passed.append(lax.ppermute(block, "row", ring))
        blocks.append(passed)

    flipped, grads, values = [], [], []
    for j in range(row_count):
        turned, kept, sent = mix(wanted, blocks[j], weight)
        if pieces > 1:
            partial_value = jnp.concatenate([kept, sent.astype(jnp.float32)])
            partial_value = partial_value.reshape(col_count, tok_rows, pieces, columns).transpose(0, 2, 1, 3)
            partial_value = partial_value.reshape(depth_count, tok_rows, columns)
            partial_value = jnp.concatenate(
                [lax.dynamic_index_in_dim(partial_value, depth ^ q, 0, keepdims=False) for q in order]
            )
            count = partial_value.shape[0] // 2
            kept, sent = partial_value[:count], partial_value[count:].astype(jnp.bfloat16)
        for bit in range(bits - 1):
            arrived = flip(sent, bit)
            kept, sent = fold(kept, arrived)
        theirs = lax.dynamic_index_in_dim(upstream, lax.rem(row + j, row_count), 0, keepdims=False)
        theirs = lax.ppermute(theirs, ("col", "depth"), away)
        gelu_value, grad = slope(kept, flip(sent, bits - 1), theirs, fan_scale)
        held = [grad]
        values.append(lax.ppermute(gelu_value, ("col", "depth"), home))
        for bit in reversed(range(bits)):
            held = held + [flip(h, bit) for h in held]
        if pieces > 1:
            stacked = jnp.stack(held)
            table = jnp.array([order.index(q) for q in range(depth_count)], jnp.int32)
            grad = jnp.stack(
                [
                    lax.dynamic_index_in_dim(stacked, table[depth ^ piece_at[t, p]], 0, keepdims=False)
                    for t in range(col_count)
                    for p in range(pieces)
                ]
            )
            grad = grad.reshape(col_count, pieces, tok_rows, columns).transpose(0, 2, 1, 3)
            held = [grad.reshape(col_count * tok_rows, pieces * columns)]
        flipped.append(turned)
        grads.append(held)
    new_weight, new_moment = lion_step(flipped, grads, weight, moment)
    twice = jnp.stack(values + values)
    activated = lax.dynamic_slice_in_dim(twice, row_count - row, row_count, axis=0)
    return (activated, new_weight, new_moment)


def solution(mesh):
    depth_count, col_count = mesh.shape["depth"], mesh.shape["col"]
    assert depth_count % col_count == 0 and depth_count & (depth_count - 1) == 0
    placed = (
        P(("row", "col"), "depth"),
        P("depth", ("row", "col")),
        P("depth", ("row", "col")),
        P(None, "col", ("row", "depth")),
    )

    return jax.shard_map(
        shards,
        mesh=mesh,
        in_specs=placed,
        out_specs=(
            P(None, "col", ("row", "depth")),
            P("depth", ("row", "col")),
            P("depth", ("row", "col")),
        ),
        check_vma=False,
    )
```

time: 160 us -> 172 us (1.075)
  waiting for transfers between devices: 48.6 us -> 70 us
  matrix products: 19.4 us -> 0 us
  starting transfers between devices: 34.5 us -> 42.2 us
  Pallas kernels: 43 us -> 50.6 us
  local copies, waits for them, and re-layouts: 7.99 us -> 4.69 us
  other arithmetic: 4.8 us -> 2.75 us
    dot_general x4 -> x0, matrix products: 19.4 us -> none  [the longest x2 12.8 us: shards(): jnp.dot(ordered[count:], near, preferred_element_type=jnp.float32)]
    pallas_call x3 -> x6, Pallas kernels: 7.91 us -> 21.4 us  [the longest x2 17.4 us: mix(): pl.pallas_call(functools.partial(mix_kernel, wanted), in_specs=[near] * l...]
    ppermute x10, starting transfers between devices: 11.5 us -> 22.6 us  [flip(): lax.ppermute(value, 'depth', [(q, q ^ 1 << bit) for q in range(depth_coun...]
    ppermute x10, waiting for transfers between devices: 33.4 us -> 42.7 us  [flip(): lax.ppermute(value, 'depth', [(q, q ^ 1 << bit) for q in range(depth_coun...]
    ppermute x10, waiting for transfers between devices: 5.36 us -> 14 us  [the longest x4 10.1 us: shards(): passed.append(lax.ppermute(block, 'row', ring))]
    pallas_call x1, Pallas kernels: 35.1 us -> 29.2 us  [lion_step(): pl.pallas_call(functools.partial(lion_kernel, (len(held), len(held[0])),...]
    ppermute x10, starting transfers between devices: 17.9 us -> 14.4 us  [the longest x4 5.13 us: shards(): passed.append(lax.ppermute(block, 'row', ring))]
    ppermute x1, waiting for transfers between devices: 0.01 us -> 3.5 us  [shards(): from_below = lax.ppermute(from_below, 'col', up)]
  transfers between devices with their start and end apart: 22 -> 22, of which waited for: 5 -> 9; matrix products, arithmetic and copies ran while one was open for 16% -> 2% of each run, Pallas kernels for 5% -> 13%
where the time goes in v3:
time: 172 us; the launch traced here: 171 us
  waiting for transfers between devices  70 us (41%)
  Pallas kernels  50.6 us (29%)
  starting transfers between devices  42.2 us (25%)
  local copies, waits for them, and re-layouts  4.69 us (3%)
  other arithmetic  2.75 us (2%)
    ppermute x10, waiting for transfers between devices, flip(): lax.ppermute(value, 'depth', [(q, q ^ 1 << bit) for q in range(depth_coun...  42.7 us
    pallas_call x1, Pallas kernels, lion_step(): pl.pallas_call(functools.partial(lion_kernel, (len(held), len(held[0])),...  29.2 us
    ppermute x10, starting transfers between devices, flip(): lax.ppermute(value, 'depth', [(q, q ^ 1 << bit) for q in range(depth_coun...  22.6 us
    pallas_call x2, Pallas kernels, mix(): pl.pallas_call(functools.partial(mix_kernel, wanted), in_specs=[near] * l...  17.4 us
    ppermute x4, waiting for transfers between devices, shards(): passed.append(lax.ppermute(block, 'row', ring))  10.1 us
    ppermute x1, waiting for transfers between devices, shards(): from_above = lax.ppermute(from_above, 'col', down)  9.82 us
    ppermute x4, starting transfers between devices, shards(): passed.append(lax.ppermute(block, 'row', ring))  5.13 us
    ppermute x1, starting transfers between devices, shards(): from_above = lax.ppermute(from_above, 'col', down)  5.13 us
  transfers between devices with their start and end apart: 22, of which 9 were waited for; matrix products, arithmetic and copies ran while one was open for 2% of the time, Pallas kernels for 13%

profile of v3, /device:TPU:0, one launch (start us, length us, event | category | flops | bytes accessed | tf_op | source)
XLA Modules:
  0.0 171.2 jit_solution(2411032253550457010)
XLA Ops:
  0.6 0.0 copy-start.4
  0.6 5.1 %collective-permute-start = (bf16[64,3072]{1,0:T(8,128)(2,1)}, bf16[64,3072]{1,0:T(8,128)(2,1)S(1)}, u32[]{:S(2)}, u32[]{:S(2)}) collective-permute-start(bf16[64,3072]{1,0:T(8,128)(2,1)} %refs_0_.1), channel_id=1, source_target_pairs={{4,0},{8,4},{12,8},{0,12},{5,1},{9,5},{13,9},{1,13},{6,2},{10,6},{... | collective-permute-start | bytes 1179656 | tf_op jit(solution)/shard_map/ppermute | solution.py:283
  5.8 0.0 collective-permute-start.2
  5.8 9.8 %collective-permute-done.refs_1_ = bf16[64,3072]{1,0:T(8,128)(2,1)S(1)} collective-permute-done((bf16[64,3072]{1,0:T(8,128)(2,1)}, bf16[64,3072]{1,0:T(8,128)(2,1)S(1)}, u32[]{:S(2)}, u32[]{:S(2)}) %collective-permute-start) | collective-permute-done | bytes 393248 | tf_op jit(solution)/shard_map/ppermute | solution.py:283
  15.6 4.2 %collective-permute-start.1 = (bf16[32,3072]{1,0:T(8,128)(2,1)S(1)}, bf16[32,3072]{1,0:T(8,128)(2,1)S(1)}, u32[]{:S(2)}, u32[]{:S(2)}) collective-permute-start(bf16[32,3072]{1,0:T(8,128)(2,1)S(1)} %slice.8), channel_id=1, source_target_pairs={{4,0},{8,4},{12,8},{0,12},{5,1},{9,5},{13,9},{1,13},{6,2},{10,6},{... | collective-permute-start | bytes 589832 | tf_op jit(solution)/shard_map/ppermute | solution.py:288
  19.8 1.5 collective-permute-start.8
  21.4 3.5 %collective-permute-done.2.refs_3_ = bf16[64,3072]{1,0:T(8,128)(2,1)S(1)} collective-permute-done((bf16[64,3072]{1,0:T(8,128)(2,1)}, bf16[64,3072]{1,0:T(8,128)(2,1)S(1)}, u32[]{:S(2)}, u32[]{:S(2)}) %collective-permute-start.2) | collective-permute-done | bytes 393248 | tf_op jit(solution)/shard_map/ppermute | solution.py:284
  24.9 1.6 collective-permute-start.3
  26.5 1.5 collective-permute-start.11
  28.0 0.5 collective-permute-start.9
  28.5 0.0 collective-permute-done.1
  28.5 3.9 %collective-permute-done.3 = bf16[32,3072]{1,0:T(8,128)(2,1)S(1)} collective-permute-done((bf16[32,3072]{1,0:T(8,128)(2,1)S(1)}, bf16[32,3072]{1,0:T(8,128)(2,1)S(1)}, u32[]{:S(2)}, u32[]{:S(2)}) %collective-permute-start.3) | collective-permute-done | bytes 196640 | tf_op jit(solution)/shard_map/ppermute | solution.py:289
  32.4 1.6 collective-permute-start.10
  34.0 0.0 copy-done.4
  34.0 8.7 %mix.2 = (bf16[3072,256]{1,0:T(8,128)(2,1)S(1)}, f32[128,3072]{1,0:T(8,128)S(1)}, bf16[128,3072]{1,0:T(8,128)(2,1)}) custom-call(bf16[64,3072]{1,0:T(8,128)(2,1)S(1)} %copy-done.4, bf16[64,3072]{1,0:T(8,128)(2,1)S(1)} %collective-permute-done.refs_1_, bf16[64,3072]{1,0:T(8,128)(2,1)S(1)} %constant_dynamic-update-slice_fusion.refs_2_, ...), custom_call_target="tpu_custom_call" | custom-call | flops 4831838208 | bytes 18874368 | tf_op jit(solution)/shard_map/mix/pallas_call | solution.py:87
  42.7 1.2 copy-done
  43.9 0.0 collective-permute-start.4
  43.9 0.0 collective-permute-done.8.refs_0_
  43.9 0.0 collective-permute-done.11.refs_3_
  43.9 3.7 %collective-permute-done.9.refs_1_ = bf16[64,3072]{1,0:T(8,128)(2,1)S(1)} collective-permute-done((bf16[64,3072]{1,0:T(8,128)(2,1)S(1)}, bf16[64,3072]{1,0:T(8,128)(2,1)S(1)}, u32[]{:S(2)}, u32[]{:S(2)}) %collective-permute-start.9) | collective-permute-done | bytes 393248 | tf_op jit(solution)/shard_map/ppermute | solution.py:295
  47.6 6.4 %collective-permute-done.10.refs_2_ = bf16[64,3072]{1,0:T(8,128)(2,1)S(1)} collective-permute-done((bf16[64,3072]{1,0:T(8,128)(2,1)S(1)}, bf16[64,3072]{1,0:T(8,128)(2,1)S(1)}, u32[]{:S(2)}, u32[]{:S(2)}) %collective-permute-start.10) | collective-permute-done | bytes 393248 | tf_op jit(solution)/shard_map/ppermute | solution.py:295
  54.0 8.7 %mix.3 = (bf16[3072,256]{1,0:T(8,128)(2,1)S(1)}, f32[128,3072]{1,0:T(8,128)S(1)}, bf16[128,3072]{1,0:T(8,128)(2,1)}) custom-call(bf16[64,3072]{1,0:T(8,128)(2,1)S(1)} %collective-permute-done.8.refs_0_, bf16[64,3072]{1,0:T(8,128)(2,1)S(1)} %collective-permute-done.9.refs_1_, bf16[64,3072]{1,0:T(8,128)(2,1)S(1)} %collective-permute-done.10.refs_2_, ...), custom_call_target="tpu_custom_call" | custom-call | flops 4831838208 | bytes 18874368 | tf_op jit(solution)/shard_map/mix/pallas_call | solution.py:87
  62.7 0.0 copy-start.1
  62.7 1.1 copy-done.1
  63.9 0.0 collective-permute-start.12
  63.9 1.2 dynamic-slice_bitcast_fusion
  65.1 0.7 collective-permute-start.6
  65.8 0.0 collective-permute-done.4.arrived
  65.8 1.3 fold.2
  67.0 2.8 %collective-permute-start.5 = (bf16[64,3072]{1,0:T(8,128)(2,1)S(1)}, bf16[64,3072]{1,0:T(8,128)(2,1)S(1)}, u32[]{:S(2)}, u32[]{:S(2)}) collective-permute-start(bf16[64,3072]{1,0:T(8,128)(2,1)S(1)} %get-tuple-element.22), channel_id=1, source_target_pairs={{0,2},{1,3},{2,0},{3,1},{4,6},{5,7},{6,4},{7,5},{8,10},{9,11},{10,... | collective-permute-start | bytes 1179656 | tf_op jit(solution)/shard_map/ppermute | solution.py:274
  69.8 0.7 collective-permute-start.14
  70.5 0.0 collective-permute-done.12.arrived
  70.5 1.3 fold.3
  71.8 4.3 %collective-permute-start.13 = (bf16[64,3072]{1,0:T(8,128)(2,1)S(1)}, bf16[64,3072]{1,0:T(8,128)(2,1)S(1)}, u32[]{:S(2)}, u32[]{:S(2)}) collective-permute-start(bf16[64,3072]{1,0:T(8,128)(2,1)S(1)} %get-tuple-element.27), channel_id=1, source_target_pairs={{0,2},{1,3},{2,0},{3,1},{4,6},{5,7},{6,4},{7,5},{8,10},{9,11},{10,... | collective-permute-start | bytes 1179656 | tf_op jit(solution)/shard_map/ppermute | solution.py:274
  76.1 0.0 collective-permute-done.6.upstream
  76.1 19.6 %collective-permute-done.5.arrived = bf16[64,3072]{1,0:T(8,128)(2,1)S(1)} collective-permute-done((bf16[64,3072]{1,0:T(8,128)(2,1)S(1)}, bf16[64,3072]{1,0:T(8,128)(2,1)S(1)}, u32[]{:S(2)}, u32[]{:S(2)}) %collective-permute-start.5) | collective-permute-done | bytes 393248 | tf_op jit(solution)/shard_map/ppermute | solution.py:274
  95.7 0.7 slope.2
  96.5 0.7 collective-permute-start.7
  97.2 3.8 %collective-permute-start.16 = (bf16[64,3072]{1,0:T(8,128)(2,1)S(1)}, bf16[64,3072]{1,0:T(8,128)(2,1)S(1)}, u32[]{:S(2)}, u32[]{:S(2)}) collective-permute-start(bf16[64,3072]{1,0:T(8,128)(2,1)S(1)} %get-tuple-element.31.refs_2_), channel_id=1, source_target_pairs={{0,2},{1,3},{2,0},{3,1},{4,6},{5,7},{6,4},{7,5},{8,10},{9,11},{10,... | collective-permute-start | bytes 1179656 | tf_op jit(solution)/shard_map/ppermute | solution.py:274
  100.9 0.0 collective-permute-done.14.upstream
  100.9 3.1 %collective-permute-done.13.arrived = bf16[64,3072]{1,0:T(8,128)(2,1)S(1)} collective-permute-done((bf16[64,3072]{1,0:T(8,128)(2,1)S(1)}, bf16[64,3072]{1,0:T(8,128)(2,1)S(1)}, u32[]{:S(2)}, u32[]{:S(2)}) %collective-permute-start.13) | collective-permute-done | bytes 393248 | tf_op jit(solution)/shard_map/ppermute | solution.py:274
  104.0 0.7 slope.3
  104.8 11.1 %collective-permute-start.19 = (bf16[64,3072]{1,0:T(8,128)(2,1)S(1)}, bf16[64,3072]{1,0:T(8,128)(2,1)S(1)}, u32[]{:S(2)}, u32[]{:S(2)}) collective-permute-start(bf16[64,3072]{1,0:T(8,128)(2,1)S(1)} %get-tuple-element.32.refs_6_), channel_id=1, source_target_pairs={{0,2},{1,3},{2,0},{3,1},{4,6},{5,7},{6,4},{7,5},{8,10},{9,11},{10,... | collective-permute-start | bytes 1179656 | tf_op jit(solution)/shard_map/ppermute | solution.py:274
  115.9 1.4 collective-permute-start.15
  117.3 0.5 collective-permute-start.17
  117.8 0.0 collective-permute-done.7
  117.8 0.1 collective-permute-start.20
  117.9 11.6 %collective-permute-done.16.refs_3_ = bf16[64,3072]{1,0:T(8,128)(2,1)S(1)} collective-permute-done((bf16[64,3072]{1,0:T(8,128)(2,1)S(1)}, bf16[64,3072]{1,0:T(8,128)(2,1)S(1)}, u32[]{:S(2)}, u32[]{:S(2)}) %collective-permute-start.16) | collective-permute-done | bytes 393248 | tf_op jit(solution)/shard_map/ppermute | solution.py:274
  129.4 0.0 collective-permute-start.18
  129.4 8.4 %collective-permute-done.19.refs_7_ = bf16[64,3072]{1,0:T(8,128)(2,1)S(1)} collective-permute-done((bf16[64,3072]{1,0:T(8,128)(2,1)S(1)}, bf16[64,3072]{1,0:T(8,128)(2,1)S(1)}, u32[]{:S(2)}, u32[]{:S(2)}) %collective-permute-start.19) | collective-permute-done | bytes 393248 | tf_op jit(solution)/shard_map/ppermute | solution.py:274
  137.9 0.0 collective-permute-start.21
  137.9 0.0 collective-permute-done.15
  137.9 2.8 %fusion.2 = bf16[2,64,3072]{2,1,0:T(8,128)(2,1)} fusion(s32[]{:T(128)S(6)} %select_n.12, bf16[1,64,3072]{2,1,0:T(8,128)(2,1)} %bitcast.6, bf16[1,64,3072]{2,1,0:T(8,128)(2,1)} %bitcast.3), kind=kLoop, calls=%fused_computation.6 | loop fusion | flops 1179648 | bytes 1572868 | tf_op jit(solution)/shard_map/stack | solution.py:335
  140.7 0.0 copy-done.2
  140.7 0.0 collective-permute-done.17.refs_4_
  140.7 0.0 collective-permute-done.20.refs_8_
  140.7 0.0 copy-start.8
  140.7 0.0 collective-permute-done.18.refs_5_
  140.7 0.0 collective-permute-done.21.refs_9_
  140.8 0.7 copy-done.7
  141.4 0.2 copy-done.8
  141.6 0.1 copy-done.9
  141.7 0.1 copy-done.10
  141.9 29.2 %lion_step.1 = (bf16[3072,3072]{1,0:T(8,128)(2,1)}, bf16[3072,3072]{1,0:T(8,128)(2,1)}) custom-call(bf16[3072,256]{1,0:T(8,128)(2,1)} %copy-done, bf16[3072,256]{1,0:T(8,128)(2,1)} %copy-done.1, bf16[64,3072]{1,0:T(8,128)(2,1)} %copy-done.2, bf16[64,3072]{1,0:T(8,128)(2,1)} %copy-done.5, bf16[64,3072]{1,0:T(8,128)(2,1)} %copy-done.7, ...), custom_call_target="tpu_custom_call" | custom-call | flops 9663676416 | bytes 75497472 | tf_op jit(solution)/shard_map/lion_step/pallas_call | solution.py:215
  (17 shorter events, 0.1 us)
Async XLA Ops:
  0.6 33.4 %copy-start.4 = (bf16[64,3072]{1,0:T(8,128)(2,1)S(1)}, bf16[64,3072]{1,0:T(8,128)(2,1)}, u32[]{:S(2)}) copy-start(bf16[64,3072]{1,0:T(8,128)(2,1)} %refs_0_.1) | copy-start | bytes 1179652
  0.6 15.0 %collective-permute-start = (bf16[64,3072]{1,0:T(8,128)(2,1)}, bf16[64,3072]{1,0:T(8,128)(2,1)S(1)}, u32[]{:S(2)}, u32[]{:S(2)}) collective-permute-start(bf16[64,3072]{1,0:T(8,128)(2,1)} %refs_0_.1), channel_id=1, source_target_pairs={{4,0},{8,4},{12,8},{0,12},{5,1},{9,5},{13,9},{1,13},{6,2},{10,6},{... | collective-permute-start | bytes 1179656 | tf_op jit(solution)/shard_map/ppermute | solution.py:283
  5.8 19.1 %collective-permute-start.2 = (bf16[64,3072]{1,0:T(8,128)(2,1)}, bf16[64,3072]{1,0:T(8,128)(2,1)S(1)}, u32[]{:S(2)}, u32[]{:S(2)}) collective-permute-start(bf16[64,3072]{1,0:T(8,128)(2,1)} %refs_0_.1), channel_id=1, source_target_pairs={{0,4},{4,8},{8,12},{12,0},{1,5},{5,9},{9,13},{13,1},{2,6},{6,10},{... | collective-permute-start | bytes 1179656 | tf_op jit(solution)/shard_map/ppermute | solution.py:284
  15.6 12.9 %collective-permute-start.1 = (bf16[32,3072]{1,0:T(8,128)(2,1)S(1)}, bf16[32,3072]{1,0:T(8,128)(2,1)S(1)}, u32[]{:S(2)}, u32[]{:S(2)}) collective-permute-start(bf16[32,3072]{1,0:T(8,128)(2,1)S(1)} %slice.8), channel_id=1, source_target_pairs={{4,0},{8,4},{12,8},{0,12},{5,1},{9,5},{13,9},{1,13},{6,2},{10,6},{... | collective-permute-start | bytes 589832 | tf_op jit(solution)/shard_map/ppermute | solution.py:288
  19.8 24.1 %collective-permute-start.8 = (bf16[64,3072]{1,0:T(8,128)(2,1)}, bf16[64,3072]{1,0:T(8,128)(2,1)S(1)}, u32[]{:S(2)}, u32[]{:S(2)}) collective-permute-start(bf16[64,3072]{1,0:T(8,128)(2,1)} %refs_0_.1), channel_id=1, source_target_pairs={{0,16},{16,0},{1,17},{17,1},{2,18},{18,2},{3,19},{19,3},{4,20},{20... | collective-permute-start | bytes 1179656 | tf_op jit(solution)/shard_map/ppermute | solution.py:295
  24.9 7.5 %collective-permute-start.3 = (bf16[32,3072]{1,0:T(8,128)(2,1)S(1)}, bf16[32,3072]{1,0:T(8,128)(2,1)S(1)}, u32[]{:S(2)}, u32[]{:S(2)}) collective-permute-start(bf16[32,3072]{1,0:T(8,128)(2,1)S(1)} %slice.9), channel_id=1, source_target_pairs={{0,4},{4,8},{8,12},{12,0},{1,5},{5,9},{9,13},{13,1},{2,6},{6,10},{... | collective-permute-start | bytes 589832 | tf_op jit(solution)/shard_map/ppermute | solution.py:289
  26.5 17.5 %collective-permute-start.11 = (bf16[64,3072]{1,0:T(8,128)(2,1)S(1)}, bf16[64,3072]{1,0:T(8,128)(2,1)S(1)}, u32[]{:S(2)}, u32[]{:S(2)}) collective-permute-start(bf16[64,3072]{1,0:T(8,128)(2,1)S(1)} %collective-permute-done.2.refs_3_), channel_id=1, source_target_pairs={{0,16},{16,0},{1,17},{17,1},{2,18},{18,2},{3,19},{19,3},{4,20},{20... | collective-permute-start | bytes 1179656 | tf_op jit(solution)/shard_map/ppermute | solution.py:295
  28.0 19.6 %collective-permute-start.9 = (bf16[64,3072]{1,0:T(8,128)(2,1)S(1)}, bf16[64,3072]{1,0:T(8,128)(2,1)S(1)}, u32[]{:S(2)}, u32[]{:S(2)}) collective-permute-start(bf16[64,3072]{1,0:T(8,128)(2,1)S(1)} %collective-permute-done.refs_1_), channel_id=1, source_target_pairs={{0,16},{16,0},{1,17},{17,1},{2,18},{18,2},{3,19},{19,3},{4,20},{20... | collective-permute-start | bytes 1179656 | tf_op jit(solution)/shard_map/ppermute | solution.py:295
  32.4 21.6 %collective-permute-start.10 = (bf16[64,3072]{1,0:T(8,128)(2,1)S(1)}, bf16[64,3072]{1,0:T(8,128)(2,1)S(1)}, u32[]{:S(2)}, u32[]{:S(2)}) collective-permute-start(bf16[64,3072]{1,0:T(8,128)(2,1)S(1)} %constant_dynamic-update-slice_fusion.refs_2_), channel_id=1, source_target_pairs={{0,16},{16,0},{1,17},{17,1},{2,18},{18,2},{3,19},{19,3},{4,20},{20... | collective-permute-start | bytes 1179656 | tf_op jit(solution)/shard_map/ppermute | solution.py:295
  42.7 1.2 copy-start
  43.9 21.8 %collective-permute-start.4 = (bf16[128,3072]{1,0:T(8,128)(2,1)}, bf16[128,3072]{1,0:T(8,128)(2,1)}, u32[]{:S(2)}, u32[]{:S(2)}) collective-permute-start(bf16[128,3072]{1,0:T(8,128)(2,1)} %get-tuple-element.20), channel_id=1, source_target_pairs={{0,1},{1,0},{2,3},{3,2},{4,5},{5,4},{6,7},{7,6},{8,9},{9,8},{10,11... | collective-permute-start | bytes 2359304 | tf_op jit(solution)/shard_map/ppermute | solution.py:274
  62.7 1.2 copy-start.1
  63.9 6.6 %collective-permute-start.12 = (bf16[128,3072]{1,0:T(8,128)(2,1)}, bf16[128,3072]{1,0:T(8,128)(2,1)}, u32[]{:S(2)}, u32[]{:S(2)}) collective-permute-start(bf16[128,3072]{1,0:T(8,128)(2,1)} %get-tuple-element.25), channel_id=1, source_target_pairs={{0,1},{1,0},{2,3},{3,2},{4,5},{5,4},{6,7},{7,6},{8,9},{9,8},{10,11... | collective-permute-start | bytes 2359304 | tf_op jit(solution)/shard_map/ppermute | solution.py:274
  65.1 11.1 %collective-permute-start.6 = (bf16[64,3072]{1,0:T(8,128)(2,1)S(1)}, bf16[64,3072]{1,0:T(8,128)(2,1)S(1)}, u32[]{:S(2)}, u32[]{:S(2)}) collective-permute-start(bf16[64,3072]{1,0:T(8,128)(2,1)S(1)} %get-tuple-element.36), channel_id=1, source_target_pairs={{0,0},{8,1},{4,2},{12,3},{1,4},{9,5},{5,6},{13,7},{2,8},{10,9},{6,... | collective-permute-start | bytes 1179656 | tf_op jit(solution)/shard_map/ppermute | solution.py:314
  67.0 28.7 %collective-permute-start.5 = (bf16[64,3072]{1,0:T(8,128)(2,1)S(1)}, bf16[64,3072]{1,0:T(8,128)(2,1)S(1)}, u32[]{:S(2)}, u32[]{:S(2)}) collective-permute-start(bf16[64,3072]{1,0:T(8,128)(2,1)S(1)} %get-tuple-element.22), channel_id=1, source_target_pairs={{0,2},{1,3},{2,0},{3,1},{4,6},{5,7},{6,4},{7,5},{8,10},{9,11},{10,... | collective-permute-start | bytes 1179656 | tf_op jit(solution)/shard_map/ppermute | solution.py:274
  69.8 31.1 %collective-permute-start.14 = (bf16[64,3072]{1,0:T(8,128)(2,1)S(1)}, bf16[64,3072]{1,0:T(8,128)(2,1)S(1)}, u32[]{:S(2)}, u32[]{:S(2)}) collective-permute-start(bf16[64,3072]{1,0:T(8,128)(2,1)S(1)} %get-tuple-element.35), channel_id=1, source_target_pairs={{0,0},{8,1},{4,2},{12,3},{1,4},{9,5},{5,6},{13,7},{2,8},{10,9},{6,... | collective-permute-start | bytes 1179656 | tf_op jit(solution)/shard_map/ppermute | solution.py:314
  71.8 32.2 %collective-permute-start.13 = (bf16[64,3072]{1,0:T(8,128)(2,1)S(1)}, bf16[64,3072]{1,0:T(8,128)(2,1)S(1)}, u32[]{:S(2)}, u32[]{:S(2)}) collective-permute-start(bf16[64,3072]{1,0:T(8,128)(2,1)S(1)} %get-tuple-element.27), channel_id=1, source_target_pairs={{0,2},{1,3},{2,0},{3,1},{4,6},{5,7},{6,4},{7,5},{8,10},{9,11},{10,... | collective-permute-start | bytes 1179656 | tf_op jit(solution)/shard_map/ppermute | solution.py:274
  96.5 44.2 %copy-start.2 = (bf16[64,3072]{1,0:T(8,128)(2,1)}, bf16[64,3072]{1,0:T(8,128)(2,1)S(1)}, u32[]{:S(2)}) copy-start(bf16[64,3072]{1,0:T(8,128)(2,1)S(1)} %get-tuple-element.31.refs_2_) | copy-start | bytes 1179652
  96.5 21.3 %collective-permute-start.7 = (bf16[64,3072]{1,0:T(8,128)(2,1)S(1)}, bf16[64,3072]{1,0:T(8,128)(2,1)S(1)}, u32[]{:S(2)}, u32[]{:S(2)}) collective-permute-start(bf16[64,3072]{1,0:T(8,128)(2,1)S(1)} %get-tuple-element.23), channel_id=1, source_target_pairs={{0,0},{1,8},{2,4},{3,12},{4,1},{5,9},{6,5},{7,13},{8,2},{9,10},{10... | collective-permute-start | bytes 1179656 | tf_op jit(solution)/shard_map/ppermute | solution.py:317
  97.2 32.3 %collective-permute-start.16 = (bf16[64,3072]{1,0:T(8,128)(2,1)S(1)}, bf16[64,3072]{1,0:T(8,128)(2,1)S(1)}, u32[]{:S(2)}, u32[]{:S(2)}) collective-permute-start(bf16[64,3072]{1,0:T(8,128)(2,1)S(1)} %get-tuple-element.31.refs_2_), channel_id=1, source_target_pairs={{0,2},{1,3},{2,0},{3,1},{4,6},{5,7},{6,4},{7,5},{8,10},{9,11},{10,... | collective-permute-start | bytes 1179656 | tf_op jit(solution)/shard_map/ppermute | solution.py:274
  104.8 36.0 %copy-start.3 = (bf16[64,3072]{1,0:T(8,128)(2,1)}, bf16[64,3072]{1,0:T(8,128)(2,1)S(1)}, u32[]{:S(2)}) copy-start(bf16[64,3072]{1,0:T(8,128)(2,1)S(1)} %get-tuple-element.32.refs_6_) | copy-start | bytes 1179652
  104.8 33.1 %collective-permute-start.19 = (bf16[64,3072]{1,0:T(8,128)(2,1)S(1)}, bf16[64,3072]{1,0:T(8,128)(2,1)S(1)}, u32[]{:S(2)}, u32[]{:S(2)}) collective-permute-start(bf16[64,3072]{1,0:T(8,128)(2,1)S(1)} %get-tuple-element.32.refs_6_), channel_id=1, source_target_pairs={{0,2},{1,3},{2,0},{3,1},{4,6},{5,7},{6,4},{7,5},{8,10},{9,11},{10,... | collective-permute-start | bytes 1179656 | tf_op jit(solution)/shard_map/ppermute | solution.py:274
  115.9 22.0 %collective-permute-start.15 = (bf16[64,3072]{1,0:T(8,128)(2,1)S(1)}, bf16[64,3072]{1,0:T(8,128)(2,1)}, u32[]{:S(2)}, u32[]{:S(2)}) collective-permute-start(bf16[64,3072]{1,0:T(8,128)(2,1)S(1)} %get-tuple-element.28), channel_id=1, source_target_pairs={{0,0},{1,8},{2,4},{3,12},{4,1},{5,9},{6,5},{7,13},{8,2},{9,10},{10... | collective-permute-start | bytes 1179656 | tf_op jit(solution)/shard_map/ppermute | solution.py:317
  117.3 23.4 %collective-permute-start.17 = (bf16[64,3072]{1,0:T(8,128)(2,1)S(1)}, bf16[64,3072]{1,0:T(8,128)(2,1)S(1)}, u32[]{:S(2)}, u32[]{:S(2)}) collective-permute-start(bf16[64,3072]{1,0:T(8,128)(2,1)S(1)} %get-tuple-element.31.refs_2_), channel_id=1, source_target_pairs={{0,1},{1,0},{2,3},{3,2},{4,5},{5,4},{6,7},{7,6},{8,9},{9,8},{10,11... | collective-permute-start | bytes 1179656 | tf_op jit(solution)/shard_map/ppermute | solution.py:274
  117.8 20.1 %copy-start.11 = (bf16[64,3072]{1,0:T(8,128)(2,1)}, bf16[64,3072]{1,0:T(8,128)(2,1)S(1)}, u32[]{:S(2)}) copy-start(bf16[64,3072]{1,0:T(8,128)(2,1)S(1)} %collective-permute-done.7) | copy-start | bytes 1179652
  117.8 22.9 %collective-permute-start.20 = (bf16[64,3072]{1,0:T(8,128)(2,1)S(1)}, bf16[64,3072]{1,0:T(8,128)(2,1)S(1)}, u32[]{:S(2)}, u32[]{:S(2)}) collective-permute-start(bf16[64,3072]{1,0:T(8,128)(2,1)S(1)} %get-tuple-element.32.refs_6_), channel_id=1, source_target_pairs={{0,1},{1,0},{2,3},{3,2},{4,5},{5,4},{6,7},{7,6},{8,9},{9,8},{10,11... | collective-permute-start | bytes 1179656 | tf_op jit(solution)/shard_map/ppermute | solution.py:274
  129.4 11.3 %copy-start.5 = (bf16[64,3072]{1,0:T(8,128)(2,1)}, bf16[64,3072]{1,0:T(8,128)(2,1)S(1)}, u32[]{:S(2)}) copy-start(bf16[64,3072]{1,0:T(8,128)(2,1)S(1)} %collective-permute-done.16.refs_3_) | copy-start | bytes 1179652
  129.4 11.3 %collective-permute-start.18 = (bf16[64,3072]{1,0:T(8,128)(2,1)S(1)}, bf16[64,3072]{1,0:T(8,128)(2,1)S(1)}, u32[]{:S(2)}, u32[]{:S(2)}) collective-permute-start(bf16[64,3072]{1,0:T(8,128)(2,1)S(1)} %collective-permute-done.16.refs_3_), channel_id=1, source_target_pairs={{0,1},{1,0},{2,3},{3,2},{4,5},{5,4},{6,7},{7,6},{8,9},{9,8},{10,11... | collective-permute-start | bytes 1179656 | tf_op jit(solution)/shard_map/ppermute | solution.py:274
  137.9 2.9 %copy-start.6 = (bf16[64,3072]{1,0:T(8,128)(2,1)}, bf16[64,3072]{1,0:T(8,128)(2,1)S(1)}, u32[]{:S(2)}) copy-start(bf16[64,3072]{1,0:T(8,128)(2,1)S(1)} %collective-permute-done.19.refs_7_) | copy-start | bytes 1179652
  137.9 2.9 %collective-permute-start.21 = (bf16[64,3072]{1,0:T(8,128)(2,1)S(1)}, bf16[64,3072]{1,0:T(8,128)(2,1)S(1)}, u32[]{:S(2)}, u32[]{:S(2)}) collective-permute-start(bf16[64,3072]{1,0:T(8,128)(2,1)S(1)} %collective-permute-done.19.refs_7_), channel_id=1, source_target_pairs={{0,1},{1,0},{2,3},{3,2},{4,5},{5,4},{6,7},{7,6},{8,9},{9,8},{10,11... | collective-permute-start | bytes 1179656 | tf_op jit(solution)/shard_map/ppermute | solution.py:274
  140.7 0.8 copy-start.7
  140.7 0.9 copy-start.8
  140.7 1.0 copy-start.9
  140.7 1.2 copy-start.10
